TPU v7x, 32 devices: a whole 2x2x4 slice. The times are simulated.
32 devices in a mesh: frames: 4 (over y, x), rows: 8 (over z, core).
Axes of the slice: x: 2, y: 2, z: 4, core: 2. Of those that a mesh axis runs over, the one named last changes fastest.
Arguments:
- inputs: bfloat16 [4, 32, 424, 256], P('frames', 'rows'), may hold values from -350 to 350, as said below
- cotangent: bfloat16 [4, 32, 424, 256], P('frames', 'rows'), may hold values from -140 to 140, as said below
- kernel: bfloat16 [3, 3, 3, 256, 256], replicated, may hold values from -0.078125 to 0.078125
- norm_gain: float32 [256], replicated, may hold values from 0.1 to 1.9
- norm_bias: float32 [256], replicated, may hold values from -1 to 1
Outputs:
- input_grad: bfloat16 [4, 32, 424, 256], P('frames', 'rows')
Inputs may be any that keep to these rules, and one draw needn't show every extreme that they name: `inputs`: finite values. `cotangent`: finite values.
All inputs are finite; a program needn't handle non-finite values.
Results may differ from a plain program's by a relative error of at most 0.0055.
Values may be sent and summed in bfloat16 or wider, within the bound.
No kernel may reach another device: no remote copies, remote signals or barrier semaphores. Data moves between devices by JAX's collectives and lax.ppermute only.
A program may use at most 64 MiB of HBM per device.

v0:
```python
import jax
import jax.numpy as jnp
from jax import lax
from jax.sharding import PartitionSpec as P

GROUPS = 32


EPS = 1e-06


def from_behind(value, axis, by):
    devices = lax.axis_size(axis)
    pairs = [(i, i + by) for i in range(devices) if 0 <= i + by < devices]
    return lax.ppermute(value, axis, pairs)


def padded_2(value, sides, width):
    for axis, dim in sides:
        devices, length = (lax.axis_size(axis), value.shape[dim])
        up = [(i, (i + 1) % devices) for i in range(devices - 1)]
        down = [(j, i) for i, j in up]
        last = lax.slice_in_dim(value, length - width, length, axis=dim)
        first = lax.slice_in_dim(value, 0, width, axis=dim)
        before = lax.ppermute(last, axis, up)
        after = lax.ppermute(first, axis, down)
        value = jnp.concatenate([before, value, after], axis=dim)
    return value


def group_sum(values):
    per_chan = jnp.sum(values, axis=(0, 1))
    return jnp.sum(per_chan.reshape(GROUPS, -1), axis=1)


def spread_groups(per_group, channels):
    return jnp.repeat(per_group, channels // GROUPS)


def transpose_conv(rimmed, flipped, strip, width, channels):
    padded = jnp.pad(rimmed, ((0, 0), (0, 0), (1, 1), (0, 0)))
    act_grad = jnp.zeros((strip, width, channels), jnp.float32)
    for row_tap in range(3):
        for col_tap in range(3):
            window = padded[
                :, 2 - row_tap : 2 - row_tap + strip, 2 - col_tap : 2 - col_tap + width, :
            ]
            act_grad = act_grad + jnp.einsum(
                "myxo,mco->yxc",
                window,
                flipped[:, row_tap, col_tap],
                preferred_element_type=jnp.float32,
            )
    return act_grad


def shards(inputs, cotangent, kernel, norm_gain, norm_bias):
    values = inputs[0].astype(jnp.float32)
    strip, width, channels = values.shape
    cells_per = (
        lax.axis_size("frames") * lax.axis_size("rows") * strip * width * (channels // GROUPS)
    )
    flipped = kernel[::-1]
    own_slab = cotangent[0]
    later = from_behind(own_slab, "frames", -1)
    latest = from_behind(own_slab, "frames", -2)
    stacked = jnp.stack([own_slab, later, latest])
    rimmed = padded_2(stacked, (("rows", 1),), 1)
    act_grad = transpose_conv(rimmed, flipped, strip, width, channels)
    totals, squares = lax.psum((group_sum(values), group_sum(values * values)), ("frames", "rows"))
    centre = totals / cells_per
    variance = jnp.maximum(squares / cells_per - centre * centre, 0.0)
    centred = values - spread_groups(centre, channels)
    inv_std = spread_groups(lax.rsqrt(variance + EPS), channels)
    normed = centred * inv_std
    preact = normed * norm_gain + norm_bias
    logistic = jax.nn.sigmoid(preact)
    norm_grad = act_grad * logistic * (1.0 + preact * (1.0 - logistic)) * norm_gain
    grad_total, grad_cross = lax.psum(
        (group_sum(norm_grad), group_sum(norm_grad * normed)), ("frames", "rows")
    )
    grad_total = grad_total / cells_per
    grad_cross = grad_cross / cells_per
    input_grad = inv_std * (
        norm_grad
        - spread_groups(grad_total, channels)
        - normed * spread_groups(grad_cross, channels)
    )
    return input_grad.astype(jnp.bfloat16)[None]


def solution(mesh):
    return jax.shard_map(
        shards,
        mesh=mesh,
        in_specs=(P("frames", "rows", None, None), P("frames", "rows", None, None), P(), P(), P()),
        out_specs=P("frames", "rows", None, None),
        check_vma=False,
    )
```

profile of v0, /device:TPU:0, one launch (start us, length us, event | category | flops | bytes accessed | tf_op | source)
XLA Modules:
  0.0 156.4 jit_solution(9935320973470033081)
XLA Ops:
  0.0 1.3 collective-permute-start.1
  1.3 1.3 collective-permute-start
  2.6 2.0 %fusion.42 = f32[256]{0:T(256)} fusion(bf16[1,4,424,256]{3,2,1,0:T(8,128)(2,1)} %param.5), kind=kLoop, calls=%fused_computation.48 | loop fusion | flops 1302272 | bytes 869376 | tf_op jit(solution)/shard_map/reduce_sum | solution.py:32
  4.6 0.9 reshape.19
  5.5 2.2 %convert_reduce_fusion = f32[256]{0:T(256)} fusion(bf16[1,4,424,256]{3,2,1,0:T(8,128)(2,1)} %param.5), kind=kLoop, calls=%fused_computation.44 | loop fusion | flops 868096 | bytes 869376 | tf_op jit(solution)/shard_map/reduce_sum | solution.py:32
  7.6 1.4 reshape.20
  9.0 0.7 reduce_sum.73
  9.7 0.8 reduce_sum.75
  10.5 67.4 %all-reduce.2 = (f32[32]{0:T(128)S(1)}, f32[32]{0:T(128)S(1)}) all-reduce(f32[32]{0:T(128)S(1)} %reduce_sum.75, f32[32]{0:T(128)} %reduce_sum.73), channel_id=1, replica_groups=mesh['frames'=4,'rows'=8] {'frames','rows'}, use_global_device_ids=true, to_apply=%region_5.6 | all-reduce | flops 64 | bytes 512 | tf_op jit(solution)/shard_map/psum | solution.py:70
  77.9 0.5 add_rsqrt_fusion
  78.4 0.1 broadcast_in_dim.18
  78.5 0.6 mul.60
  79.1 0.7 broadcast_in_dim.19
  79.8 0.6 sub.30
  80.5 0.0 collective-permute-done.1
  80.5 0.0 collective-permute-done
  80.5 2.6 %pad_maximum_fusion = (bf16[3,1,424,256]{3,2,0,1:T(8,128)(2,1)}, bf16[3,1,424,256]{3,2,0,1:T(8,128)(2,1)}) fusion(bf16[1,4,424,256]{3,2,0,1:T(8,128)(2,1)} %bitcast.5, bf16[1,4,424,256]{3,2,0,1:T(8,128)(2,1)} %bitcast.4, bf16[1,4,424,256]{3,2,0,1:T(8,128)(2,1)} %bitcast.148), kind=kLoop, calls=%fused_computation.76 | loop fusion | flops 1302528 | bytes 3907584 | tf_op jit(solution)/shard_map/slice | solution.py:24
  83.1 1.3 collective-permute-start.3
  84.3 3.9 %collective-permute-start.2 = (bf16[3,1,424,256]{3,2,0,1:T(8,128)(2,1)}, bf16[3,1,424,256]{3,2,0,1:T(8,128)(2,1)}, u32[]{:S(2)}, u32[]{:S(2)}) collective-permute-start(bf16[3,1,424,256]{3,2,0,1:T(8,128)(2,1)} %get-tuple-element.21), channel_id=1, source_target_pairs={{0,1},{1,2},{2,3},{3,4},{4,5},{5,6},{6,7},{8,9},{9,10},{10,11},{11... | collective-permute-start | bytes 1953800 | tf_op jit(solution)/shard_map/ppermute | solution.py:25
  88.2 0.0 copy-done.1
  88.2 1.9 %fusion.77 = (bf16[3,1,1,256,256]{4,3,2,1,0:T(8,128)(2,1)}, bf16[3,1,1,256,256]{4,3,2,1,0:T(8,128)(2,1)}, bf16[3,1,1,256,256]{4,3,2,1,0:T(8,128)(2,1)}, bf16[3,1...) fusion(bf16[3,3,3,256,256]{4,3,2,1,0:T(8,128)(2,1)S(1)} %copy-d, ...), kind=kLoop, calls=%fused_computation.95 | loop fusion | bytes 7077888 | tf_op jit(solution)/shard_map/slice | solution.py:51
  90.1 0.0 copy-start.5
  90.1 0.0 copy-start.4
  90.1 1.9 %slice.117 = bf16[3,1,1,256,256]{4,3,2,1,0:T(8,128)(2,1)} reverse(bf16[3,1,1,256,256]{4,3,2,1,0:T(8,128)(2,1)} %get-tuple-element.11), dimensions={0} | reverse | bytes 786432 | tf_op jit(solution)/shard_map/slice | solution.py:51
  92.0 1.8 %slice.111 = bf16[3,1,1,256,256]{4,3,2,1,0:T(8,128)(2,1)} reverse(bf16[3,1,1,256,256]{4,3,2,1,0:T(8,128)(2,1)} %get-tuple-element.12), dimensions={0} | reverse | bytes 786432 | tf_op jit(solution)/shard_map/slice | solution.py:51
  93.8 1.8 %slice.108 = bf16[3,1,1,256,256]{4,3,2,1,0:T(8,128)(2,1)} reverse(bf16[3,1,1,256,256]{4,3,2,1,0:T(8,128)(2,1)} %get-tuple-element.13), dimensions={0} | reverse | bytes 786432 | tf_op jit(solution)/shard_map/slice | solution.py:51
  95.7 0.0 copy-done.8
  95.7 0.8 slice.105
  96.5 0.0 copy-done.7
  96.5 0.0 copy-done.6
  96.5 0.0 copy-done.5
  96.6 0.0 copy-done.4
  96.6 0.8 slice.114
  97.4 0.0 copy-done.2
  97.4 2.4 %fusion.34 = f32[4,424,256,1]{2,1,3,0:T(8,128)S(1)} fusion(bf16[1,4,424,256]{3,2,0,1:T(8,128)(2,1)} %bitcast.5, bf16[1,4,424,256]{3,2,0,1:T(8,128)(2,1)} %bitcast.4, bf16[1,4,424,256]{3,2,0,1:T(8,128)(2,1)S(1)} %bitcast.149, bf16[3,1,1,256,256]{4,3,2,1,0:T(8,128)(2,1)} %slice.105), kind=kOutput, calls=%fused_computation.38 | convolution fusion | flops 669499392 | bytes 4734976 | tf_op jit(solution)/shard_map/myxo,mco->yxc/dot_general | solution.py:48
  99.9 0.0 collective-permute-done.3
  99.9 0.0 collective-permute-done.2
  99.9 4.5 %select_maximum_fusion = bf16[3,6,426,256]{3,2,0,1:T(8,128)(2,1)S(1)} fusion(bf16[3,1,424,256]{3,2,0,1:T(8,128)(2,1)} %collective-permute-done.3, bf16[3,1,424,256]{3,2,0,1:T(8,128)(2,1)} %collective-permute-done.2, bf16[1,4,424,256]{3,2,0,1:T(8,128)(2,1)} %bitcast.5, bf16[1,4,424,256]{3,2,0,1:T(8,128)(2,1)} %bitcast.4, bf16[1,4,424,256]{3,2,0,1:T(8,128)(2,1)S(1)} %bitcast.150), kind=kLoop, calls=%fused_computation.3 | loop fusion | flops 35334144 | bytes 7833600 | tf_op jit(solution)/shard_map/concatenate | solution.py:27
  104.4 1.0 fusion.24
  105.4 0.0 copy-done.11
  105.4 0.9 fusion.26
  106.3 1.0 fusion.28
  107.3 0.9 fusion.30
  108.3 1.0 fusion.32
  109.3 0.0 copy-done.12
  109.3 2.4 %fusion.14 = f32[4,424,256,1]{2,1,3,0:T(8,128)S(1)} fusion(bf16[1,4,424,256]{3,2,0,1:T(8,128)(2,1)} %bitcast.5, bf16[1,4,424,256]{3,2,0,1:T(8,128)(2,1)} %bitcast.4, bf16[1,4,424,256]{3,2,0,1:T(8,128)(2,1)S(1)} %bitcast.151, bf16[3,1,424,256]{3,2,0,1:T(8,128)(2,1)} %collective-permute-done.2, bf16[3,1,1,256,256]{4,3,2,1,0:T(8,128)(2,1)S(1)} %copy-done.12), kind=kOutput, calls=%fused_computation.18 | convolution fusion | flops 679919616 | bytes 5386240 | tf_op jit(solution)/shard_map/myxo,mco->yxc/dot_general | solution.py:48
  111.6 0.0 copy-start
  111.6 0.0 copy-start.9
  111.7 0.0 copy-start.13
  111.7 0.0 copy-start.14
  111.7 0.0 copy-start.15
  111.7 0.0 copy-start.16
  111.7 2.5 %fusion.6 = f32[4,424,256,1]{2,1,3,0:T(8,128)S(1)} fusion(bf16[3,1,424,256]{3,2,0,1:T(8,128)(2,1)} %collective-permute-done.3, bf16[1,4,424,256]{3,2,0,1:T(8,128)(2,1)} %bitcast.5, bf16[1,4,424,256]{3,2,0,1:T(8,128)(2,1)} %bitcast.4, bf16[1,4,424,256]{3,2,0,1:T(8,128)(2,1)S(1)} %bitcast.152, bf16[3,1,1,256,256]{4,3,2,1,0:T(8,128)(2,1)S(1)} %slice.97), kind=kOutput, calls=%fused_computation.10 | convolution fusion | flops 679919616 | bytes 5386240 | tf_op jit(solution)/shard_map/myxo,mco->yxc/dot_general | solution.py:48
  114.2 2.1 %fusion.76 = (f32[256]{0:T(256)S(1)}, f32[256]{0:T(256)S(1)}, f32[4,424,256]{2,1,0:T(8,128)S(1)}) fusion(f32[256]{0:T(256)S(1)} %copy-done.13, f32[256]{0:T(256)S(1)} %copy-done.14, bf16[1,4,424,256]{3,2,1,0:T(8,128)(2,1)S(1)} %copy-done, f32[256]{0:T(256)S(1)} %copy-done.15, f32[256]{0:T(256)S(1)} %copy-done.16, ...), kind=kOutput, calls=%fused_computation.94 | convolution fusion | flops 677748224 | bytes 19503104 | tf_op jit(solution)/shard_map/myxo,mco->yxc/dot_general | solution.py:48
  116.3 0.1 reshape.21
  116.4 0.1 reduce_sum.77
  116.5 0.1 reshape.22
  116.6 0.1 reduce_sum.79
  116.7 38.0 %all-reduce.1 = (f32[32]{0:T(128)S(1)}, f32[32]{0:T(128)S(1)}) all-reduce(f32[32]{0:T(128)S(1)} %reduce_sum.79, f32[32]{0:T(128)S(1)} %reduce_sum.77), channel_id=1, replica_groups=mesh['frames'=4,'rows'=8] {'frames','rows'}, use_global_device_ids=true, to_apply=%region_11.12 | all-reduce | flops 64 | bytes 512 | tf_op jit(solution)/shard_map/psum | solution.py:79
  154.8 0.1 broadcast_in_dim.21
  154.8 0.1 mul.70
  154.9 0.1 broadcast_in_dim.20
  155.0 0.1 sub.34
  155.1 1.3 fusion.63
  (22 shorter events, 0.1 us)
Async XLA Ops:
  0.0 80.5 %collective-permute-start.1 = (bf16[4,424,256]{2,1,0:T(8,128)(2,1)}, bf16[4,424,256]{2,1,0:T(8,128)(2,1)}, u32[]{:S(2)}, u32[]{:S(2)}) collective-permute-start(bf16[4,424,256]{2,1,0:T(8,128)(2,1)} %bitcast.146), channel_id=1, source_target_pairs={{16,0},{24,8},{17,1},{25,9},{18,2},{26,10},{19,3},{27,11},{20,4},{... | collective-permute-start | bytes 2605064 | tf_op jit(solution)/shard_map/ppermute | solution.py:15
  1.3 79.2 %collective-permute-start = (bf16[4,424,256]{2,1,0:T(8,128)(2,1)}, bf16[4,424,256]{2,1,0:T(8,128)(2,1)}, u32[]{:S(2)}, u32[]{:S(2)}) collective-permute-start(bf16[4,424,256]{2,1,0:T(8,128)(2,1)} %bitcast.147), channel_id=1, source_target_pairs={{8,0},{16,8},{24,16},{9,1},{17,9},{25,17},{10,2},{18,10},{26,18},{... | collective-permute-start | bytes 2605064 | tf_op jit(solution)/shard_map/ppermute | solution.py:15
  4.6 83.7 %copy-start.1 = (bf16[3,3,3,256,256]{4,3,2,1,0:T(8,128)(2,1)S(1)}, bf16[3,3,3,256,256]{4,3,2,1,0:T(8,128)(2,1)}, u32[]{:S(2)}) copy-start(bf16[3,3,3,256,256]{4,3,2,1,0:T(8,128)(2,1)} %param.7) | copy-start | bytes 10616836
  83.1 16.8 %collective-permute-start.3 = (bf16[3,1,424,256]{3,2,0,1:T(8,128)(2,1)}, bf16[3,1,424,256]{3,2,0,1:T(8,128)(2,1)}, u32[]{:S(2)}, u32[]{:S(2)}) collective-permute-start(bf16[3,1,424,256]{3,2,0,1:T(8,128)(2,1)} %get-tuple-element.20), channel_id=1, source_target_pairs={{1,0},{2,1},{3,2},{4,3},{5,4},{6,5},{7,6},{9,8},{10,9},{11,10},{12... | collective-permute-start | bytes 1953800 | tf_op jit(solution)/shard_map/ppermute | solution.py:26
  84.3 15.5 %collective-permute-start.2 = (bf16[3,1,424,256]{3,2,0,1:T(8,128)(2,1)}, bf16[3,1,424,256]{3,2,0,1:T(8,128)(2,1)}, u32[]{:S(2)}, u32[]{:S(2)}) collective-permute-start(bf16[3,1,424,256]{3,2,0,1:T(8,128)(2,1)} %get-tuple-element.21), channel_id=1, source_target_pairs={{0,1},{1,2},{2,3},{3,4},{4,5},{5,6},{6,7},{8,9},{9,10},{10,11},{11... | collective-permute-start | bytes 1953800 | tf_op jit(solution)/shard_map/ppermute | solution.py:25
  90.1 5.6 %copy-start.8 = (bf16[3,1,1,256,256]{4,3,2,1,0:T(8,128)(2,1)S(1)}, bf16[3,1,1,256,256]{4,3,2,1,0:T(8,128)(2,1)}, u32[]{:S(2)}) copy-start(bf16[3,1,1,256,256]{4,3,2,1,0:T(8,128)(2,1)} %get-tuple-element.14) | copy-start | bytes 1179652
  90.1 6.4 %copy-start.7 = (bf16[3,1,1,256,256]{4,3,2,1,0:T(8,128)(2,1)S(1)}, bf16[3,1,1,256,256]{4,3,2,1,0:T(8,128)(2,1)}, u32[]{:S(2)}) copy-start(bf16[3,1,1,256,256]{4,3,2,1,0:T(8,128)(2,1)} %get-tuple-element.15) | copy-start | bytes 1179652
  90.1 6.4 %copy-start.6 = (bf16[3,1,1,256,256]{4,3,2,1,0:T(8,128)(2,1)S(1)}, bf16[3,1,1,256,256]{4,3,2,1,0:T(8,128)(2,1)}, u32[]{:S(2)}) copy-start(bf16[3,1,1,256,256]{4,3,2,1,0:T(8,128)(2,1)} %get-tuple-element.16) | copy-start | bytes 1179652
  90.1 6.5 %copy-start.5 = (bf16[3,1,1,256,256]{4,3,2,1,0:T(8,128)(2,1)S(1)}, bf16[3,1,1,256,256]{4,3,2,1,0:T(8,128)(2,1)}, u32[]{:S(2)}) copy-start(bf16[3,1,1,256,256]{4,3,2,1,0:T(8,128)(2,1)} %get-tuple-element.17) | copy-start | bytes 1179652
  90.1 6.5 %copy-start.4 = (bf16[3,1,1,256,256]{4,3,2,1,0:T(8,128)(2,1)S(1)}, bf16[3,1,1,256,256]{4,3,2,1,0:T(8,128)(2,1)}, u32[]{:S(2)}) copy-start(bf16[3,1,1,256,256]{4,3,2,1,0:T(8,128)(2,1)} %get-tuple-element.18) | copy-start | bytes 1179652
  92.0 4.6 %copy-start.3 = (bf16[3,1,1,256,256]{4,3,2,1,0:T(8,128)(2,1)S(1)}, bf16[3,1,1,256,256]{4,3,2,1,0:T(8,128)(2,1)}, u32[]{:S(2)}) copy-start(bf16[3,1,1,256,256]{4,3,2,1,0:T(8,128)(2,1)} %get-tuple-element.19) | copy-start | bytes 1179652
  93.8 3.6 %copy-start.2 = (bf16[1,4,424,256]{3,2,1,0:T(8,128)(2,1)S(1)}, bf16[1,4,424,256]{3,2,1,0:T(8,128)(2,1)}, u32[]{:S(2)}) copy-start(bf16[1,4,424,256]{3,2,1,0:T(8,128)(2,1)} %param.6) | copy-start | bytes 2605060
  99.8 4.5 %copy-start.10 = (bf16[3,1,1,256,256]{4,3,2,1,0:T(8,128)(2,1)S(1)}, bf16[3,1,1,256,256]{4,3,2,1,0:T(8,128)(2,1)}, u32[]{:S(2)}) copy-start(bf16[3,1,1,256,256]{4,3,2,1,0:T(8,128)(2,1)} %slice.111) | copy-start | bytes 1179652
  104.4 1.0 copy-start.11
  108.3 1.0 copy-start.12
  111.6 2.5 %copy-start = (bf16[1,4,424,256]{3,2,1,0:T(8,128)(2,1)S(1)}, bf16[1,4,424,256]{3,2,1,0:T(8,128)(2,1)}, u32[]{:S(2)}) copy-start(bf16[1,4,424,256]{3,2,1,0:T(8,128)(2,1)} %param.5) | copy-start | bytes 2605060
  111.6 2.5 %copy-start.9 = (bf16[3,1,1,256,256]{4,3,2,1,0:T(8,128)(2,1)S(1)}, bf16[3,1,1,256,256]{4,3,2,1,0:T(8,128)(2,1)}, u32[]{:S(2)}) copy-start(bf16[3,1,1,256,256]{4,3,2,1,0:T(8,128)(2,1)} %slice.117) | copy-start | bytes 1179652
  111.7 2.5 %copy-start.13 = (f32[256]{0:T(256)S(1)}, f32[256]{0:T(256)}, u32[]{:S(2)}) copy-start(f32[256]{0:T(256)} %mul.60) | copy-start | bytes 3076
  111.7 2.5 %copy-start.14 = (f32[256]{0:T(256)S(1)}, f32[256]{0:T(256)}, u32[]{:S(2)}) copy-start(f32[256]{0:T(256)} %sub.30) | copy-start | bytes 3076
  111.7 2.5 %copy-start.15 = (f32[256]{0:T(256)S(1)}, f32[256]{0:T(256)}, u32[]{:S(2)}) copy-start(f32[256]{0:T(256)} %param.9) | copy-start | bytes 3076
  111.7 2.5 %copy-start.16 = (f32[256]{0:T(256)S(1)}, f32[256]{0:T(256)}, u32[]{:S(2)}) copy-start(f32[256]{0:T(256)} %param.8) | copy-start | bytes 3076
where the time goes:
time: 157 us; the launch traced here: 156 us
  blocking collectives  105 us (67%)
  other arithmetic  14.9 us (9%)
  matrix products  14.1 us (9%)
  local copies, waits for them, and re-layouts  14 us (9%)
  starting transfers between devices  7.73 us (5%)
    psum x1, blocking collectives, shards(): lax.psum((group_sum(values), group_sum(values * values)), ('frames', 'row...  67.4 us
    psum x1, blocking collectives, shards(): lax.psum((group_sum(norm_grad), group_sum(norm_grad * normed)), ('frames'...  38 us
    dot_general x9, matrix products, transpose_conv(): jnp.einsum('myxo,mco->yxc', window, flipped[:, row_tap, col_tap], preferr...  14.1 us
    slice x10, local copies, waits for them, and re-layouts, transpose_conv(): flipped[:, row_tap, col_tap]  9.11 us
    concatenate x1, other arithmetic, padded_2(): value = jnp.concatenate([before, value, after], axis=dim)  4.5 us
    reduce_sum x2, other arithmetic, group_sum(): per_chan = jnp.sum(values, axis=(0, 1))  4.14 us
    ppermute x1, starting transfers between devices, padded_2(): before = lax.ppermute(last, axis, up)  3.87 us
  transfers between devices with their start and end apart: 4, of which 0 were waited for; matrix products, arithmetic and copies ran while one was open for 14% of the time, Pallas kernels for 0%

commit v1 on v0

v1 whole, which is shorter than its diff:
```python
import functools
import jax
import jax.numpy as jnp
from jax import lax
from jax.experimental import pallas as pl
from jax.experimental.pallas import tpu as pltpu
from jax.sharding import PartitionSpec as P

GROUPS = 32
EPS = 1e-06
F32 = jnp.float32
BF16 = jnp.bfloat16
HIGH = lax.Precision.HIGHEST
VMEM = pl.BlockSpec(memory_space=pltpu.VMEM)
LIMIT = 60 * 1024 * 1024


def call(body, out_shape, flops, moved, in_specs=None, **kw):
    return pl.pallas_call(
        body,
        out_shape=out_shape,
        cost_estimate=pl.CostEstimate(flops=flops, bytes_accessed=moved, transcendentals=0),
        compiler_params=pltpu.CompilerParams(vmem_limit_bytes=LIMIT),
        **({} if in_specs is None else {"in_specs": in_specs}),
        **kw,
    )


def membership(channels, lanes, flip):
    per = channels // GROUPS
    shape = (lanes, channels) if flip else (channels, lanes)
    chan = lax.broadcasted_iota(jnp.int32, shape, 1 if flip else 0)
    lane = lax.broadcasted_iota(jnp.int32, shape, 0 if flip else 1)
    return (chan // per == lane).astype(F32)


def pack_sums(first, second, out_ref):
    channels = first.shape[-1]
    row = lax.broadcasted_iota(jnp.int32, (8, channels), 0)
    both = jnp.where(row == 0, first, jnp.where(row == 1, second, 0.0))
    sums = jnp.dot(both, membership(channels, 128, False), precision=HIGH, preferred_element_type=F32)
    out_ref[...] = jnp.broadcast_to(sums[None], out_ref.shape)


def unpack_sums(got_ref, channels, cells):
    total = jnp.sum(got_ref[...], axis=0) / cells
    wide = jnp.dot(total, membership(channels, 128, True), precision=HIGH, preferred_element_type=F32)
    return wide, total


def stats_body(x_ref, out_ref):
    v = x_ref[0].astype(F32)
    v = v.reshape(-1, v.shape[-1])
    pack_sums(jnp.sum(v, axis=0, keepdims=True), jnp.sum(v * v, axis=0, keepdims=True), out_ref)


def norm_params(got_ref, channels, cells):
    total = jnp.sum(got_ref[...], axis=0) / cells
    centre, square = total[0:1], total[1:2]
    variance = jnp.maximum(square - centre * centre, 0.0)
    inv_std = lax.rsqrt(variance + EPS)
    row = lax.broadcasted_iota(jnp.int32, (8, 128), 0)
    both = jnp.where(row == 0, centre, jnp.where(row == 1, inv_std, 0.0))
    wide = jnp.dot(both, membership(channels, 128, True), precision=HIGH, preferred_element_type=F32)
    return wide[0:1], wide[1:2]


def taps(lhs, w):
    return lax.dot_general(lhs, w, (((1,), (1,)), ((), ())), preferred_element_type=F32)


def columns(a):
    width, wide = a.shape
    c = wide // 3
    at = lax.broadcasted_iota(jnp.int32, (width, c), 0)
    left = pltpu.roll(a[:, :c], width - 1, 0)
    right = pltpu.roll(a[:, 2 * c :], 1, 0)
    left = jnp.where(at == width - 1, 0.0, left)
    right = jnp.where(at == 0, 0.0, right)
    return a[:, c : 2 * c] + left + right


def weights(w_ref, row_tap, frame_taps):
    c = w_ref.shape[-1]
    parts = [w_ref[k, row_tap].reshape(3 * c, c) for k in frame_taps]
    return parts[0] if len(parts) == 1 else jnp.concatenate(parts, axis=1)


def own_body(f_ref, w_ref, acc_ref):
    _, strip, width, c = f_ref.shape
    ws = [w_ref[0, i].reshape(3 * c, c) for i in range(3)]
    for y in range(-1, strip + 1):
        rows = [(y + 1 - i, i) for i in range(3) if 0 <= y + 1 - i < strip]
        lhs = jnp.concatenate([f_ref[0, r] for r, _ in rows], axis=1)
        w = jnp.concatenate([ws[i] for _, i in rows], axis=1)
        acc_ref[y + 1] = columns(taps(lhs, w))


def border_body(xl_ref, dl_ref, lt_ref, w_ref, acc_ref, out_ref, up_ref, down_ref):
    strip, width, c = xl_ref.shape
    ends = (0, strip - 1)
    lhs = [
        jnp.concatenate([xl_ref[r] + dl_ref[n], lt_ref[n]], axis=1) for n, r in enumerate(ends)
    ]
    for i in range(3):
        w = jnp.concatenate([w_ref[1, i].reshape(3 * c, c), w_ref[0, i].reshape(3 * c, c)], axis=1)
        for n, r in enumerate(ends):
            y = r - 1 + i
            value = acc_ref[y + 1] + columns(taps(lhs[n], w))
            if y == -1:
                up_ref[...] = value.astype(BF16)
            elif y == strip:
                down_ref[...] = value.astype(BF16)
            else:
                out_ref[y] = value


def inner_conv(rows, w_ref, acc, strip, put):
    c = w_ref.shape[-1]
    ws = [w_ref[0, i].reshape(3 * c, c) for i in range(3)]
    for y in range(strip):
        use = [(y + 1 - i, i) for i in range(3) if 1 <= y + 1 - i < strip - 1]
        lhs = jnp.concatenate([rows[r - 1] for r, _ in use], axis=1)
        w = jnp.concatenate([ws[i] for _, i in use], axis=1)
        put(y, acc[y] + columns(taps(lhs, w)))


def inner_body(xl_ref, rl_ref, w_ref, acc_ref, out_ref):
    strip = acc_ref.shape[0]
    rows = [xl_ref[r] + rl_ref[r - 1] for r in range(1, strip - 1)]

    def put(y, value):
        out_ref[y] = value

    inner_conv(rows, w_ref, acc_ref, strip, put)


def last_body(
    cells, a_ref, b_ref, w_ref, acc_ref, above_ref, below_ref, x_ref, got_ref, gain_ref, bias_ref,
    grad_ref, sums_ref,
):
    strip, _, c = acc_ref.shape
    rows = [a_ref[r] + b_ref[r] for r in range(strip - 2)]
    centre, inv_std = norm_params(got_ref, c, cells)
    gain, bias = gain_ref[...], bias_ref[...]
    sums = [jnp.zeros((1, c), F32), jnp.zeros((1, c), F32)]

    def put(y, value):
        if y == 0:
            value = value + above_ref[...].astype(F32)
        if y == strip - 1:
            value = value + below_ref[...].astype(F32)
        normed = (x_ref[0, y].astype(F32) - centre) * inv_std
        preact = normed * gain + bias
        logistic = jax.nn.sigmoid(preact)
        grad = value * logistic * (1.0 + preact * (1.0 - logistic)) * gain
        grad_ref[y] = grad
        sums[0] = sums[0] + jnp.sum(grad, axis=0, keepdims=True)
        sums[1] = sums[1] + jnp.sum(grad * normed, axis=0, keepdims=True)

    inner_conv(rows, w_ref, acc_ref, strip, put)
    pack_sums(sums[0], sums[1], sums_ref)


def final_body(cells, grad_ref, x_ref, got_ref, sums_ref, out_ref):
    strip, _, c = grad_ref.shape
    centre, inv_std = norm_params(got_ref, c, cells)
    wide, _ = unpack_sums(sums_ref, c, cells)
    total, cross = wide[0:1], wide[1:2]
    for y in range(strip):
        normed = (x_ref[0, y].astype(F32) - centre) * inv_std
        value = inv_std * (grad_ref[y] - total - normed * cross)
        out_ref[0, y] = value.astype(BF16)


def shards(inputs, cotangent, kernel, norm_gain, norm_bias):
    _, strip, width, c = inputs.shape
    frames, lines = lax.axis_size("frames"), lax.axis_size("rows")
    devices = frames * lines
    cells = float(devices * strip * width * (c // GROUPS))
    slab = cotangent[0]
    inner = slab[1 : strip - 1]
    ends = jnp.concatenate([slab[:1], slab[strip - 1 :]])

    def move(value, pairs):
        return lax.ppermute(value, "frames", pairs)

    def two(keep):
        return [(i, i - 2) for i in range(2, frames) if keep(i)]

    even, odd = (lambda i: i % 2 == 0), (lambda i: i % 2 == 1)
    later_x = move(slab, [(i, i - 1) for i in range(1, frames, 2)])
    latest_in_even = move(inner, two(even))
    later_ends = move(ends, [(i, i - 1) for i in range(2, frames, 2)])
    latest_ends = move(ends, two(lambda i: True))
    latest_in_odd = move(inner, two(odd))
    later_in = move(latest_in_even, [(i, i + 1) for i in range(0, frames - 2, 2)])

    row_f32 = jax.ShapeDtypeStruct((strip, width, c), F32)
    row_b16 = jax.ShapeDtypeStruct((width, c), BF16)
    sums_shape = jax.ShapeDtypeStruct((devices, 8, 128), F32)
    tap = 2 * width * c * c * 3
    size = width * c

    def swap(sums):
        return lax.all_to_all(sums, ("frames", "rows"), 0, 0, tiled=True)

    got = swap(call(stats_body, sums_shape, 8 * strip * size, 2 * strip * size)(inputs))

    def kspec(start, count):
        return pl.BlockSpec((count, 3, 3, c, c), lambda g: (start // count, 0, 0, 0, 0))

    def full(shape):
        return pl.BlockSpec(shape, lambda g: (0,) * len(shape))

    def conv_call(body, shapes, out_shapes, wspec, at, flops, moved):
        specs = [full(s) for s in shapes]
        specs.insert(at, wspec)
        one = not isinstance(out_shapes, (list, tuple))
        outs = full(out_shapes.shape) if one else [full(o.shape) for o in out_shapes]
        return call(
            body, out_shapes, flops, moved, in_specs=specs, out_specs=outs, grid=(1,)
        )

    acc6 = jax.ShapeDtypeStruct((strip + 2, width, c), F32)
    whole, pair, line = (strip, width, c), (strip - 2, width, c), (width, c)
    own = conv_call(own_body, [cotangent.shape], acc6, kspec(2, 1), 1, tap * 3 * strip, 8 * 6 * size)(
        cotangent, kernel
    )
    acc, up, down = conv_call(
        border_body, [whole, (2, width, c), (2, width, c), acc6.shape], [row_f32, row_b16, row_b16],
        kspec(0, 2), 3, tap * 12, 8 * 16 * size,
    )(later_x, later_ends, latest_ends, kernel, own)
    to_next = [(i, i + 1) for i in range(lines - 1)]
    to_prev = [(i + 1, i) for i in range(lines - 1)]
    above = lax.ppermute(down, "rows", to_next)
    below = lax.ppermute(up, "rows", to_prev)
    acc = conv_call(inner_body, [whole, pair, whole], row_f32, kspec(1, 1), 2, tap * 6, 8 * 12 * size)(
        later_x, later_in, kernel, acc
    )
    vec = norm_gain.reshape(1, c), norm_bias.reshape(1, c)
    grad, sums = conv_call(
        functools.partial(last_body, cells),
        [pair, pair, whole, line, line, inputs.shape, sums_shape.shape, (1, c), (1, c)],
        [row_f32, sums_shape], kspec(0, 1), 2, tap * 6, 8 * 12 * size,
    )(latest_in_even, latest_in_odd, kernel, acc, above, below, inputs, got, *vec)
    sums = swap(sums)
    return call(
        functools.partial(final_body, cells), jax.ShapeDtypeStruct(inputs.shape, BF16),
        10 * strip * size, 8 * strip * size,
    )(grad, inputs, got, sums)


def solution(mesh):
    return jax.shard_map(
        shards,
        mesh=mesh,
        in_specs=(P("frames", "rows", None, None), P("frames", "rows", None, None), P(), P(), P()),
        out_specs=P("frames", "rows", None, None),
        check_vma=False,
    )
```

time: 157 us -> 73.9 us (0.47)
  blocking collectives: 105 us -> 17 us
  Pallas kernels: 0 us -> 27.8 us
  starting transfers between devices: 7.73 us -> 23 us
  other arithmetic: 14.9 us -> 0.04 us
  matrix products: 14.1 us -> 0 us
  local copies, waits for them, and re-layouts: 14 us -> 5.45 us
    psum x2 -> x0, blocking collectives: 105 us -> none  [the longest x1 67.4 us: shards(): lax.psum((group_sum(values), group_sum(values * values)), ('frames', 'row...]
    pallas_call x0 -> x6, Pallas kernels: none -> 27.8 us  [the longest x1 6.31 us: shards(): conv_call(border_body, [whole, (2, width, c), (2, width, c), acc6.shape],...]
    all_to_all x0 -> x1, blocking collectives: none -> 17 us  [swap(): return lax.all_to_all(sums, ('frames', 'rows'), 0, 0, tiled=True)]
    dot_general x9 -> x0, matrix products: 14.1 us -> none  [transpose_conv(): jnp.einsum('myxo,mco->yxc', window, flipped[:, row_tap, col_tap], preferr...]
    all_to_all x0 -> x1, starting transfers between devices: none -> 11 us  [swap(): return lax.all_to_all(sums, ('frames', 'rows'), 0, 0, tiled=True)]
    slice x10 -> x2, local copies, waits for them, and re-layouts: 9.11 us -> 2.11 us  [the longest x1 1.07 us: shards(): ends = jnp.concatenate([slab[:1], slab[strip - 1:]])]
    reduce_sum x6 -> x0, other arithmetic: 5.91 us -> none  [the longest x2 4.14 us: group_sum(): per_chan = jnp.sum(values, axis=(0, 1))]
    concatenate x1, other arithmetic: 4.5 us -> 0.04 us  [shards(): ends = jnp.concatenate([slab[:1], slab[strip - 1:]])]
  transfers between devices with their start and end apart: 4 -> 9, of which waited for: 0 -> 0; matrix products, arithmetic and copies ran while one was open for 14% -> 3% of each run, Pallas kernels for 0% -> 25%
where the time goes in v1:
time: 73.9 us; the launch traced here: 73.4 us
  Pallas kernels  27.8 us (38%)
  starting transfers between devices  23 us (31%)
  blocking collectives  17 us (23%)
  local copies, waits for them, and re-layouts  5.45 us (7%)
    all_to_all x1, blocking collectives, swap(): return lax.all_to_all(sums, ('frames', 'rows'), 0, 0, tiled=True)  17 us
    all_to_all x1, starting transfers between devices, swap(): return lax.all_to_all(sums, ('frames', 'rows'), 0, 0, tiled=True)  11 us
    ppermute x6, starting transfers between devices, move(): return lax.ppermute(value, 'frames', pairs)  8.94 us
    pallas_call x1, Pallas kernels, shards(): conv_call(border_body, [whole, (2, width, c), (2, width, c), acc6.shape],...  6.31 us
    pallas_call x1, Pallas kernels, shards(): conv_call(functools.partial(last_body, cells), [pair, pair, whole, line,...  5.57 us
    pallas_call x1, Pallas kernels, shards(): conv_call(own_body, [cotangent.shape], acc6, kspec(2, 1), 1, tap * 3 * st...  5.3 us
    pallas_call x1, Pallas kernels, shards(): conv_call(inner_body, [whole, pair, whole], row_f32, kspec(1, 1), 2, tap...  4.72 us
    pallas_call x1, Pallas kernels, shards(): call(functools.partial(final_body, cells), jax.ShapeDtypeStruct(inputs.sh...  3.64 us
  transfers between devices with their start and end apart: 9, of which 0 were waited for; matrix products, arithmetic and copies ran while one was open for 3% of the time, Pallas kernels for 25%

profile of v1, /device:TPU:0, one launch (start us, length us, event | category | flops | bytes accessed | tf_op | source)
XLA Modules:
  0.0 73.4 jit_solution(14186290294317823246)
XLA Ops:
  0.0 1.3 %collective-permute-start.2 = (bf16[4,424,256]{2,1,0:T(8,128)(2,1)}, bf16[4,424,256]{2,1,0:T(8,128)(2,1)S(1)}, u32[]{:S(2)}, u32[]{:S(2)}) collective-permute-start(bf16[4,424,256]{2,1,0:T(8,128)(2,1)} %bitcast.9), channel_id=1, source_target_pairs={{8,0},{24,16},{9,1},{25,17},{10,2},{26,18},{11,3},{27,19},{12,4},{... | collective-permute-start | bytes 2605064 | tf_op jit(solution)/shard_map/ppermute | solution.py:186
  1.3 1.0 %slice_bitcast_fusion = bf16[2,424,256]{2,1,0:T(8,128)(2,1)S(1)} fusion(bf16[1,4,424,256]{3,2,1,0:T(8,128)(2,1)} %f_ref.1), kind=kLoop, calls=%fused_computation.1 | loop fusion | bytes 868352 | tf_op jit(solution)/shard_map/slice | solution.py:182
  2.3 1.3 %collective-permute-start = (bf16[2,424,256]{2,1,0:T(8,128)(2,1)S(1)}, bf16[2,424,256]{2,1,0:T(8,128)(2,1)S(1)}, u32[]{:S(2)}, u32[]{:S(2)}) collective-permute-start(bf16[2,424,256]{2,1,0:T(8,128)(2,1)S(1)} %slice_bitcast_fusion), channel_id=1, source_target_pairs={{16,0},{17,1},{18,2},{19,3},{20,4},{21,5},{22,6},{23,7}} | collective-permute-start | bytes 1302536 | tf_op jit(solution)/shard_map/ppermute | solution.py:186
  3.6 1.1 %slice_bitcast_fusion.2 = (bf16[1,424,256]{2,1,0:T(8,128)(2,1)S(1)}, bf16[1,424,256]{2,1,0:T(8,128)(2,1)S(1)}) fusion(bf16[1,4,424,256]{3,2,1,0:T(8,128)(2,1)} %f_ref.1), kind=kLoop, calls=%fused_computation.3 | loop fusion | bytes 868352 | tf_op jit(solution)/shard_map/slice | solution.py:183
  4.8 0.7 collective-permute-start.4
  5.5 1.3 %collective-permute-start.5 = (bf16[2,424,256]{2,1,0:T(8,128)(2,1)S(1)}, bf16[2,424,256]{2,1,0:T(8,128)(2,1)}, u32[]{:S(2)}, u32[]{:S(2)}) collective-permute-start(bf16[2,424,256]{2,1,0:T(8,128)(2,1)S(1)} %pad_maximum_fusion), channel_id=1, source_target_pairs={{16,0},{24,8},{17,1},{25,9},{18,2},{26,10},{19,3},{27,11},{20,4},{... | collective-permute-start | bytes 1302536 | tf_op jit(solution)/shard_map/ppermute | solution.py:186
  6.8 0.7 collective-permute-start.1
  7.5 2.2 %shard_map.58 = f32[32,8,128]{2,1,0:T(8,128)} custom-call(bf16[1,4,424,256]{3,2,1,0:T(8,128)(2,1)} %x_ref.5), custom_call_target="tpu_custom_call" | custom-call | flops 3473408 | bytes 868352 | tf_op jit(solution)/shard_map/pallas_call | solution.py:208
  9.7 11.0 %all-to-all-start = ((f32[32,8,128]{2,1,0:T(8,128)}), f32[32,8,128]{2,1,0:T(8,128)S(1)}, u32[]{:S(2)}, u32[]{:S(2)}) async-start(f32[32,8,128]{2,1,0:T(8,128)} %shard_map.58), calls=%async_computation | async-start | bytes 262144 | tf_op jit(solution)/shard_map/all_to_all | solution.py:206
  20.7 0.0 collective-permute-done.a_ref
  20.7 0.0 copy-start.2
  20.7 3.7 %collective-permute-start.3 = (bf16[2,424,256]{2,1,0:T(8,128)(2,1)S(1)}, bf16[2,424,256]{2,1,0:T(8,128)(2,1)S(1)}, u32[]{:S(2)}, u32[]{:S(2)}) collective-permute-start(bf16[2,424,256]{2,1,0:T(8,128)(2,1)S(1)} %collective-permute-done.a_ref), channel_id=1, source_target_pairs={{0,8},{1,9},{2,10},{3,11},{4,12},{5,13},{6,14},{7,15}} | collective-permute-start | bytes 1302536 | tf_op jit(solution)/shard_map/ppermute | solution.py:186
  24.4 5.3 %shard_map.55.acc_ref = f32[6,424,256]{2,1,0:T(8,128)} custom-call(bf16[1,4,424,256]{3,2,1,0:T(8,128)(2,1)} %f_ref.1, bf16[3,3,3,256,256]{4,3,2,1,0:T(8,128)(2,1)} %w_ref.7), custom_call_target="tpu_custom_call" | custom-call | flops 2000683008 | bytes 5210112 | tf_op jit(solution)/shard_map/pallas_call | solution.py:227
  29.7 0.0 copy-done.2
  29.7 0.0 collective-permute-done.4.dl_ref
  29.8 0.0 copy-start.5
  29.8 0.0 collective-permute-done.5.lt_ref
  29.8 0.0 collective-permute-done.2.xl_ref
  29.8 0.8 %copy-done.5 = bf16[2,424,256]{2,1,0:T(8,128)(2,1)} copy-done((bf16[2,424,256]{2,1,0:T(8,128)(2,1)}, bf16[2,424,256]{2,1,0:T(8,128)(2,1)S(1)}, u32[]{:S(2)}) %copy-start.5) | copy-done | bytes 434200
  30.5 0.0 copy-start
  30.6 0.9 %copy-done = bf16[4,424,256]{2,1,0:T(8,128)(2,1)} copy-done((bf16[4,424,256]{2,1,0:T(8,128)(2,1)}, bf16[4,424,256]{2,1,0:T(8,128)(2,1)S(1)}, u32[]{:S(2)}) %copy-start) | copy-done | bytes 868376
  31.5 6.3 %shard_map.56 = (f32[4,424,256]{2,1,0:T(8,128)}, bf16[424,256]{1,0:T(8,128)(2,1)}, bf16[424,256]{1,0:T(8,128)(2,1)}) custom-call(bf16[4,424,256]{2,1,0:T(8,128)(2,1)} %copy-done, bf16[2,424,256]{2,1,0:T(8,128)(2,1)} %copy-done.5, bf16[2,424,256]{2,1,0:T(8,128)(2,1)} %collective-permute-done.5.lt_ref, bf16[3,3,3,256,256]{4,3,2,1,0:T(8,128)(2,1)} %w_ref.7, ...), custom_call_target="tpu_custom_call" | custom-call | flops 2000683008 | bytes 13893632 | tf_op jit(solution)/shard_map/pallas_call | solution.py:230
  37.8 1.7 %collective-permute-start.6 = (bf16[424,256]{1,0:T(8,128)(2,1)}, bf16[424,256]{1,0:T(8,128)(2,1)S(1)}, u32[]{:S(2)}, u32[]{:S(2)}) collective-permute-start(bf16[424,256]{1,0:T(8,128)(2,1)} %get-tuple-element.11), channel_id=1, source_target_pairs={{0,1},{1,2},{2,3},{3,4},{4,5},{5,6},{6,7},{8,9},{9,10},{10,11},{11... | collective-permute-start | bytes 651272 | tf_op jit(solution)/shard_map/ppermute | solution.py:236
  39.5 1.3 %collective-permute-start.7 = (bf16[424,256]{1,0:T(8,128)(2,1)}, bf16[424,256]{1,0:T(8,128)(2,1)S(1)}, u32[]{:S(2)}, u32[]{:S(2)}) collective-permute-start(bf16[424,256]{1,0:T(8,128)(2,1)} %get-tuple-element.12), channel_id=1, source_target_pairs={{1,0},{2,1},{3,2},{4,3},{5,4},{6,5},{7,6},{9,8},{10,9},{11,10},{12... | collective-permute-start | bytes 651272 | tf_op jit(solution)/shard_map/ppermute | solution.py:237
  40.8 0.0 collective-permute-done.3.rl_ref
  40.8 0.0 copy-start.4
  40.8 0.8 %copy-done.4 = bf16[2,424,256]{2,1,0:T(8,128)(2,1)} copy-done((bf16[2,424,256]{2,1,0:T(8,128)(2,1)}, bf16[2,424,256]{2,1,0:T(8,128)(2,1)S(1)}, u32[]{:S(2)}) %copy-start.4) | copy-done | bytes 434200
  41.6 4.7 %shard_map.57.acc_ref = f32[4,424,256]{2,1,0:T(8,128)} custom-call(bf16[4,424,256]{2,1,0:T(8,128)(2,1)} %copy-done, bf16[2,424,256]{2,1,0:T(8,128)(2,1)} %copy-done.4, bf16[3,3,3,256,256]{4,3,2,1,0:T(8,128)(2,1)} %w_ref.7, f32[4,424,256]{2,1,0:T(8,128)} %get-tuple-element.10.acc_ref), custom_call_target="tpu_custom_call" | custom-call | flops 1000341504 | bytes 10420224 | tf_op jit(solution)/shard_map/pallas_call | solution.py:238
  46.3 0.0 all-to-all-done.got_ref
  46.3 0.0 copy-start.1
  46.3 0.0 collective-permute-done.1.b_ref
  46.3 0.0 copy-start.3
  46.3 0.0 collective-permute-done.6.above_ref
  46.4 0.0 copy-start.6
  46.4 0.0 collective-permute-done.7.below_ref
  46.4 0.0 copy-start.7
  46.4 0.6 copy-done.1
  47.0 0.2 copy-done.3
  47.1 0.1 copy-done.6
  47.2 0.1 copy-done.7
  47.3 5.6 %shard_map.59 = (f32[4,424,256]{2,1,0:T(8,128)}, f32[32,8,128]{2,1,0:T(8,128)}) custom-call(bf16[2,424,256]{2,1,0:T(8,128)(2,1)} %copy-done.2, bf16[2,424,256]{2,1,0:T(8,128)(2,1)} %copy-done.3, bf16[3,3,3,256,256]{4,3,2,1,0:T(8,128)(2,1)} %w_ref.7, f32[4,424,256]{2,1,0:T(8,128)} %shard_map.57.acc_ref, bf16[424,256]{1,0:T(8,128)(2,1)} %copy-done.6, ...), custom_call_target="tpu_custom_call" | custom-call | flops 1000341504 | bytes 10420224 | tf_op jit(solution)/shard_map/pallas_call | solution.py:242
  52.8 17.0 %all_to_all.10.sums_ref = f32[32,8,128]{2,1,0:T(8,128)} all-to-all(f32[32,8,128]{2,1,0:T(8,128)} %get-tuple-element.14), channel_id=1, replica_groups=mesh['frames'=4,'rows'=8] {'frames','rows'}, dimensions={0} | all-to-all | bytes 262144 | tf_op jit(solution)/shard_map/all_to_all | solution.py:206
  69.8 3.6 %shard_map.60 = bf16[1,4,424,256]{3,2,1,0:T(8,128)(2,1)} custom-call(f32[4,424,256]{2,1,0:T(8,128)} %get-tuple-element.13.grad_ref, bf16[1,4,424,256]{3,2,1,0:T(8,128)(2,1)} %x_ref.5, f32[32,8,128]{2,1,0:T(8,128)} %copy-done.1, f32[32,8,128]{2,1,0:T(8,128)} %all_to_all.10.sums_ref), custom_call_target="tpu_custom_call" | custom-call | flops 4341760 | bytes 3473408 | tf_op jit(solution)/shard_map/pallas_call | solution.py:248
  (1 shorter events, 0.0 us)
Async XLA Ops:
  0.0 29.8 %collective-permute-start.2 = (bf16[4,424,256]{2,1,0:T(8,128)(2,1)}, bf16[4,424,256]{2,1,0:T(8,128)(2,1)S(1)}, u32[]{:S(2)}, u32[]{:S(2)}) collective-permute-start(bf16[4,424,256]{2,1,0:T(8,128)(2,1)} %bitcast.9), channel_id=1, source_target_pairs={{8,0},{24,16},{9,1},{25,17},{10,2},{26,18},{11,3},{27,19},{12,4},{... | collective-permute-start | bytes 2605064 | tf_op jit(solution)/shard_map/ppermute | solution.py:186
  2.3 18.4 %collective-permute-start = (bf16[2,424,256]{2,1,0:T(8,128)(2,1)S(1)}, bf16[2,424,256]{2,1,0:T(8,128)(2,1)S(1)}, u32[]{:S(2)}, u32[]{:S(2)}) collective-permute-start(bf16[2,424,256]{2,1,0:T(8,128)(2,1)S(1)} %slice_bitcast_fusion), channel_id=1, source_target_pairs={{16,0},{17,1},{18,2},{19,3},{20,4},{21,5},{22,6},{23,7}} | collective-permute-start | bytes 1302536 | tf_op jit(solution)/shard_map/ppermute | solution.py:186
  4.8 25.0 %collective-permute-start.4 = (bf16[2,424,256]{2,1,0:T(8,128)(2,1)S(1)}, bf16[2,424,256]{2,1,0:T(8,128)(2,1)S(1)}, u32[]{:S(2)}, u32[]{:S(2)}) collective-permute-start(bf16[2,424,256]{2,1,0:T(8,128)(2,1)S(1)} %pad_maximum_fusion), channel_id=1, source_target_pairs={{16,8},{17,9},{18,10},{19,11},{20,12},{21,13},{22,14},{23,15}} | collective-permute-start | bytes 1302536 | tf_op jit(solution)/shard_map/ppermute | solution.py:186
  5.5 24.3 %collective-permute-start.5 = (bf16[2,424,256]{2,1,0:T(8,128)(2,1)S(1)}, bf16[2,424,256]{2,1,0:T(8,128)(2,1)}, u32[]{:S(2)}, u32[]{:S(2)}) collective-permute-start(bf16[2,424,256]{2,1,0:T(8,128)(2,1)S(1)} %pad_maximum_fusion), channel_id=1, source_target_pairs={{16,0},{24,8},{17,1},{25,9},{18,2},{26,10},{19,3},{27,11},{20,4},{... | collective-permute-start | bytes 1302536 | tf_op jit(solution)/shard_map/ppermute | solution.py:186
  6.8 39.6 %collective-permute-start.1 = (bf16[2,424,256]{2,1,0:T(8,128)(2,1)S(1)}, bf16[2,424,256]{2,1,0:T(8,128)(2,1)S(1)}, u32[]{:S(2)}, u32[]{:S(2)}) collective-permute-start(bf16[2,424,256]{2,1,0:T(8,128)(2,1)S(1)} %slice_bitcast_fusion), channel_id=1, source_target_pairs={{24,8},{25,9},{26,10},{27,11},{28,12},{29,13},{30,14},{31,15}} | collective-permute-start | bytes 1302536 | tf_op jit(solution)/shard_map/ppermute | solution.py:186
  9.7 36.7 %all-to-all-start = ((f32[32,8,128]{2,1,0:T(8,128)}), f32[32,8,128]{2,1,0:T(8,128)S(1)}, u32[]{:S(2)}, u32[]{:S(2)}) async-start(f32[32,8,128]{2,1,0:T(8,128)} %shard_map.58), calls=%async_computation | async-start | bytes 262144 | tf_op jit(solution)/shard_map/all_to_all | solution.py:206
  20.7 9.0 %copy-start.2 = (bf16[2,424,256]{2,1,0:T(8,128)(2,1)}, bf16[2,424,256]{2,1,0:T(8,128)(2,1)S(1)}, u32[]{:S(2)}) copy-start(bf16[2,424,256]{2,1,0:T(8,128)(2,1)S(1)} %collective-permute-done.a_ref) | copy-start | bytes 1302532
  20.7 20.1 %collective-permute-start.3 = (bf16[2,424,256]{2,1,0:T(8,128)(2,1)S(1)}, bf16[2,424,256]{2,1,0:T(8,128)(2,1)S(1)}, u32[]{:S(2)}, u32[]{:S(2)}) collective-permute-start(bf16[2,424,256]{2,1,0:T(8,128)(2,1)S(1)} %collective-permute-done.a_ref), channel_id=1, source_target_pairs={{0,8},{1,9},{2,10},{3,11},{4,12},{5,13},{6,14},{7,15}} | collective-permute-start | bytes 1302536 | tf_op jit(solution)/shard_map/ppermute | solution.py:186
  29.8 0.8 %copy-start.5 = (bf16[2,424,256]{2,1,0:T(8,128)(2,1)}, bf16[2,424,256]{2,1,0:T(8,128)(2,1)S(1)}, u32[]{:S(2)}) copy-start(bf16[2,424,256]{2,1,0:T(8,128)(2,1)S(1)} %collective-permute-done.4.dl_ref) | copy-start | bytes 1302532
  30.5 0.9 %copy-start = (bf16[4,424,256]{2,1,0:T(8,128)(2,1)}, bf16[4,424,256]{2,1,0:T(8,128)(2,1)S(1)}, u32[]{:S(2)}) copy-start(bf16[4,424,256]{2,1,0:T(8,128)(2,1)S(1)} %collective-permute-done.2.xl_ref) | copy-start | bytes 2605060
  37.8 8.6 %collective-permute-start.6 = (bf16[424,256]{1,0:T(8,128)(2,1)}, bf16[424,256]{1,0:T(8,128)(2,1)S(1)}, u32[]{:S(2)}, u32[]{:S(2)}) collective-permute-start(bf16[424,256]{1,0:T(8,128)(2,1)} %get-tuple-element.11), channel_id=1, source_target_pairs={{0,1},{1,2},{2,3},{3,4},{4,5},{5,6},{6,7},{8,9},{9,10},{10,11},{11... | collective-permute-start | bytes 651272 | tf_op jit(solution)/shard_map/ppermute | solution.py:236
  39.5 6.9 %collective-permute-start.7 = (bf16[424,256]{1,0:T(8,128)(2,1)}, bf16[424,256]{1,0:T(8,128)(2,1)S(1)}, u32[]{:S(2)}, u32[]{:S(2)}) collective-permute-start(bf16[424,256]{1,0:T(8,128)(2,1)} %get-tuple-element.12), channel_id=1, source_target_pairs={{1,0},{2,1},{3,2},{4,3},{5,4},{6,5},{7,6},{9,8},{10,9},{11,10},{12... | collective-permute-start | bytes 651272 | tf_op jit(solution)/shard_map/ppermute | solution.py:237
  40.8 0.8 %copy-start.4 = (bf16[2,424,256]{2,1,0:T(8,128)(2,1)}, bf16[2,424,256]{2,1,0:T(8,128)(2,1)S(1)}, u32[]{:S(2)}) copy-start(bf16[2,424,256]{2,1,0:T(8,128)(2,1)S(1)} %collective-permute-done.3.rl_ref) | copy-start | bytes 1302532
  46.3 0.6 copy-start.1
  46.3 0.8 %copy-start.3 = (bf16[2,424,256]{2,1,0:T(8,128)(2,1)}, bf16[2,424,256]{2,1,0:T(8,128)(2,1)S(1)}, u32[]{:S(2)}) copy-start(bf16[2,424,256]{2,1,0:T(8,128)(2,1)S(1)} %collective-permute-done.1.b_ref) | copy-start | bytes 1302532
  46.4 0.8 %copy-start.6 = (bf16[424,256]{1,0:T(8,128)(2,1)}, bf16[424,256]{1,0:T(8,128)(2,1)S(1)}, u32[]{:S(2)}) copy-start(bf16[424,256]{1,0:T(8,128)(2,1)S(1)} %collective-permute-done.6.above_ref) | copy-start | bytes 651268
  46.4 0.9 %copy-start.7 = (bf16[424,256]{1,0:T(8,128)(2,1)}, bf16[424,256]{1,0:T(8,128)(2,1)S(1)}, u32[]{:S(2)}) copy-start(bf16[424,256]{1,0:T(8,128)(2,1)S(1)} %collective-permute-done.7.below_ref) | copy-start | bytes 651268

commit v2 on v0

v2 whole, which is shorter than its diff:
```python
import functools
import jax
import jax.numpy as jnp
from jax import lax
from jax.experimental import pallas as pl
from jax.experimental.pallas import tpu as pltpu
from jax.sharding import PartitionSpec as P

GROUPS = 32
EPS = 1e-06
F32 = jnp.float32
BF16 = jnp.bfloat16
HIGH = lax.Precision.HIGHEST
DMA = pltpu.SemaphoreType.DMA
LIMIT = 24 * 1024 * 1024


def call(body, outs, flops, moved, args, near=(), far=(), scratch=()):
    spaces = [pltpu.VMEM if n in near else pltpu.HBM if n in far else None for n in range(len(args))]
    return pl.pallas_call(
        body,
        out_shape=outs,
        in_specs=[pl.BlockSpec(memory_space=m or pl.ANY) for m in spaces],
        out_specs=[
            pl.BlockSpec(memory_space=pltpu.HBM if isinstance(o, jax.ShapeDtypeStruct) else pltpu.VMEM)
            for o in outs
        ],
        scratch_shapes=list(scratch),
        cost_estimate=pl.CostEstimate(flops=flops, bytes_accessed=moved, transcendentals=0),
        compiler_params=pltpu.CompilerParams(vmem_limit_bytes=LIMIT),
    )(*(v if m is None else pltpu.with_memory_space_constraint(v, m) for v, m in zip(args, spaces)))


def fetch(sems, *pairs):
    copies = [pltpu.make_async_copy(a, b, sems.at[n]) for n, (a, b) in enumerate(pairs)]
    for copy in copies:
        copy.start()
    return copies


def same_group(channels):
    per = channels // GROUPS
    one = lax.broadcasted_iota(jnp.int32, (channels, channels), 0) // per
    two = lax.broadcasted_iota(jnp.int32, (channels, channels), 1) // per
    return (one == two).astype(F32)


def pack_sums(first, second, out_ref):
    channels = first.shape[-1]
    row = lax.broadcasted_iota(jnp.int32, (8, channels), 0)
    both = jnp.where(row == 0, first, jnp.where(row == 1, second, 0.0))
    sums = jnp.dot(both, same_group(channels), precision=HIGH, preferred_element_type=F32)
    out_ref[...] = jnp.broadcast_to(sums[None, 0:2], out_ref.shape)


def stats_body(x_ref, out_ref, near, sems):
    _, strip, _, c = x_ref.shape
    copies = fetch(sems, *((x_ref.at[0, y], near.at[y]) for y in range(strip)))
    first, second = jnp.zeros((1, c), F32), jnp.zeros((1, c), F32)
    for y in range(strip):
        copies[y].wait()
        v = near[y].astype(F32)
        first = first + jnp.sum(v, axis=0, keepdims=True)
        second = second + jnp.sum(v * v, axis=0, keepdims=True)
    pack_sums(first, second, out_ref)


def taps(lhs, w):
    return lax.dot_general(lhs, w, (((1,), (1,)), ((), ())), preferred_element_type=F32)


def columns(a):
    width, wide = a.shape
    c = wide // 3
    at = lax.broadcasted_iota(jnp.int32, (width, c), 0)
    left = pltpu.roll(a[:, :c], width - 1, 0)
    right = pltpu.roll(a[:, 2 * c :], 1, 0)
    left = jnp.where(at == width - 1, 0.0, left)
    right = jnp.where(at == 0, 0.0, right)
    return a[:, c : 2 * c] + left + right


def flat(w_ref, frame_tap, row_tap):
    c = w_ref.shape[-1]
    return w_ref[frame_tap, row_tap].reshape(3 * c, c)


def own_body(slab_ref, far_ref, acc_ref, w_ref, slab, sems):
    _, strip, _, _ = slab_ref.shape
    copies = fetch(
        sems, (slab_ref.at[0], slab), (far_ref.at[2], w_ref.at[2]),
        (far_ref.at[1], w_ref.at[1]), (far_ref.at[0], w_ref.at[0]),
    )
    copies[0].wait()
    copies[1].wait()
    for y in range(-1, strip + 1):
        rows = [(y + 1 - i, i) for i in range(3) if 0 <= y + 1 - i < strip]
        lhs = jnp.concatenate([slab[r] for r, _ in rows], axis=1)
        w = jnp.concatenate([flat(w_ref, 2, i) for _, i in rows], axis=1)
        acc_ref[y + 1] = columns(taps(lhs, w))
    copies[2].wait()
    copies[3].wait()


def border_body(
    xl_ref, dl_ref, le_ref, lo_ref, w_ref, acc_ref, out_ref, mate_ref, other_ref, xl, dl, le, lo, sems
):
    strip, _, _ = xl_ref.shape
    ends = (0, strip - 1)
    odd = lax.axis_index("rows") % 2
    copies = fetch(
        sems, *((xl_ref.at[r], xl.at[n]) for n, r in enumerate(ends)),
        *((le_ref.at[r], le.at[n]) for n, r in enumerate(ends)),
        *((lo_ref.at[r], lo.at[n]) for n, r in enumerate(ends)), (dl_ref, dl),
    )
    for copy in copies:
        copy.wait()
    lhs = [jnp.concatenate([xl[n] + dl[n], le[n] + lo[n]], axis=1) for n in range(2)]
    for i in (0, 2, 1):
        w = jnp.concatenate([flat(w_ref, 1, i), flat(w_ref, 0, i)], axis=1)
        for n, r in enumerate(ends):
            y = r - 1 + i
            value = acc_ref[y + 1] + columns(taps(lhs[n], w))
            if 0 <= y < strip:
                out_ref[y] = value
                continue
            value = value.astype(BF16)

            @pl.when(odd == (1 if y == -1 else 0))
            def _():
                mate_ref[...] = value

            @pl.when(odd == (0 if y == -1 else 1))
            def _():
                other_ref[...] = value


def inner_body(xl_ref, rl_ref, le_ref, lo_ref, w_ref, acc_ref, out_ref, xl, rl, le, lo, sems):
    strip = acc_ref.shape[0]
    copies = fetch(
        sems, (xl_ref.at[1 : strip - 1], xl), (rl_ref, rl), (le_ref.at[1 : strip - 1], le),
        (lo_ref.at[1 : strip - 1], lo),
    )
    for copy in copies:
        copy.wait()
    frames = [jnp.concatenate([xl[r] + rl[r], le[r] + lo[r]], axis=1) for r in range(strip - 2)]
    for y in range(strip):
        use = [(y + 1 - i, i) for i in range(3) if 1 <= y + 1 - i < strip - 1]
        lhs = jnp.concatenate([frames[r - 1] for r, _ in use], axis=1)
        w = jnp.concatenate([flat(w_ref, k, i) for _, i in use for k in (1, 0)], axis=1)
        out_ref[y] = acc_ref[y] + columns(taps(lhs, w))


def last_body(
    cells, acc_ref, mate_ref, other_ref, far_x_ref, gain_ref, bias_ref, got_ref,
    grad_ref, x_ref, params_ref, sums_ref, mate, other, gains, biases, got, sems,
):
    strip, _, c = acc_ref.shape
    odd = lax.axis_index("rows") % 2
    copies = fetch(
        sems, (got_ref, got), (gain_ref, gains), (bias_ref, biases), (mate_ref, mate), (other_ref, other),
        *((far_x_ref.at[0, y], x_ref.at[y]) for y in range(strip)),
    )
    for copy in copies[:3]:
        copy.wait()
    total = jnp.sum(got[...], axis=0) / cells
    centre = total[0:1]
    variance = jnp.maximum(total[1:2] - centre * centre, 0.0)
    inv_std = lax.rsqrt(variance + EPS)
    params_ref[0:1] = centre
    params_ref[1:2] = inv_std
    gain, bias = gains[...], biases[...]
    first, second = jnp.zeros((1, c), F32), jnp.zeros((1, c), F32)
    for copy in copies[3:]:
        copy.wait()
    for y in range(strip):
        value = acc_ref[y]
        if y in (0, strip - 1):
            from_mate = odd == (1 if y == 0 else 0)
            value = value + jnp.where(from_mate, mate[...].astype(F32), other[...].astype(F32))
        normed = (x_ref[y].astype(F32) - centre) * inv_std
        preact = normed * gain + bias
        logistic = jax.nn.sigmoid(preact)
        grad = value * (logistic * (1.0 + preact * (1.0 - logistic)) * gain)
        grad_ref[y] = grad
        first = first + jnp.sum(grad, axis=0, keepdims=True)
        second = second + jnp.sum(grad * normed, axis=0, keepdims=True)
    pack_sums(first, second, sums_ref)


def final_body(cells, grad_ref, x_ref, params_ref, sums_ref, out_ref, rows, sems):
    strip, _, _ = grad_ref.shape
    centre, inv_std = params_ref[0:1], params_ref[1:2]
    means = jnp.sum(sums_ref[...], axis=0) / cells
    total, cross = means[0:1], means[1:2]
    copies = []
    for y in range(strip):
        normed = (x_ref[y].astype(F32) - centre) * inv_std
        value = inv_std * (grad_ref[y] - total - normed * cross)
        rows[y] = value.astype(BF16)
        copies.append(pltpu.make_async_copy(rows.at[y], out_ref.at[0, y], sems.at[y]))
        copies[-1].start()
    for copy in copies:
        copy.wait()


def shards(inputs, cotangent, kernel, norm_gain, norm_bias):
    _, strip, width, c = inputs.shape
    frames, lines = lax.axis_size("frames"), lax.axis_size("rows")
    devices = frames * lines
    cells = float(devices * strip * width * (c // GROUPS))
    size = width * c
    tap = 2 * size * c * 3
    whole, pair, line = (strip, width, c), (strip - 2, width, c), (width, c)
    near = lambda shape, kind=F32: pltpu.VMEM(shape, kind)
    sums_shape = near((devices, 2, c))
    slab = cotangent[0]

    def move(value, pairs, axis="frames"):
        return lax.ppermute(value, axis, pairs)

    def swap(sums):
        return lax.all_to_all(sums, ("frames", "rows"), 0, 0, tiled=True)

    latest_odd = move(slab, [(i, i - 2) for i in range(3, frames, 2)])
    latest_even = move(slab, [(i, i - 2) for i in range(2, frames, 2)])
    later_x = move(slab, [(i, i - 1) for i in range(1, frames, 2)])
    ends = jnp.concatenate([slab[:1], slab[strip - 1 :]])
    later_ends = move(ends, [(i, i - 1) for i in range(2, frames, 2)])
    later_in = move(latest_even[1 : strip - 1], [(i, i + 1) for i in range(0, frames - 2, 2)])

    (sums,) = call(
        stats_body, [sums_shape], 8 * strip * size, 2 * strip * size, (inputs,), far=(0,),
        scratch=[near(whole, BF16), DMA((strip,))],
    )
    got = swap(sums)
    acc, w = call(
        own_body, [near((strip + 2, width, c)), near(kernel.shape, BF16)],
        tap * 3 * strip, 8 * 6 * size, (cotangent, kernel), far=(0, 1), scratch=[near(whole, BF16), DMA((4,))],
    )
    acc, mate, other = call(
        border_body, [near(whole), near(line, BF16), near(line, BF16)], tap * 12, 8 * 16 * size,
        (later_x, later_ends, latest_even, latest_odd, w, acc), near=(4, 5),
        scratch=[near((2, width, c), BF16)] * 4 + [DMA((7,))],
    )
    mate = move(mate, [(i, i ^ 1) for i in range(lines)], "rows")
    between = [(i, i + 1) for i in range(1, lines - 1, 2)]
    other = move(other, between + [(j, i) for i, j in between], "rows")
    (acc,) = call(
        inner_body, [near(whole)], tap * 12, 8 * 12 * size, (later_x, later_in, latest_even, latest_odd, w, acc),
        near=(4, 5), scratch=[near(pair, BF16)] * 4 + [DMA((4,))],
    )
    grad, x, params, sums = call(
        functools.partial(last_body, cells), [near(whole), near(whole, BF16), near((8, c)), sums_shape],
        40 * strip * size, 8 * 4 * size,
        (acc, mate, other, inputs, norm_gain.reshape(1, c), norm_bias.reshape(1, c), got),
        near=(0,), far=(3, 4, 5),
        scratch=[near(line, BF16), near(line, BF16), near((1, c)), near((1, c)), near((devices, 2, c)),
                 DMA((5 + strip,))],
    )
    sums = swap(sums)
    (out,) = call(
        functools.partial(final_body, cells), [jax.ShapeDtypeStruct(inputs.shape, BF16)],
        10 * strip * size, 8 * strip * size, (grad, x, params, sums), near=(0, 1, 2, 3),
        scratch=[near(whole, BF16), DMA((strip,))],
    )
    return out


def solution(mesh):
    return jax.shard_map(
        shards,
        mesh=mesh,
        in_specs=(P("frames", "rows", None, None), P("frames", "rows", None, None), P(), P(), P()),
        out_specs=P("frames", "rows", None, None),
        check_vma=False,
    )
```

time: 157 us -> 82.8 us (0.53)
  blocking collectives: 105 us -> 13 us
  waiting for transfers between devices: 0.01 us -> 18.7 us
  Pallas kernels: 0 us -> 18.6 us
  other arithmetic: 14.9 us -> 0.04 us
  matrix products: 14.1 us -> 0 us
  starting transfers between devices: 7.73 us -> 20.4 us
  local copies, waits for them, and re-layouts: 14 us -> 11.4 us
    psum x2 -> x0, blocking collectives: 105 us -> none  [the longest x1 67.4 us: shards(): lax.psum((group_sum(values), group_sum(values * values)), ('frames', 'row...]
    ppermute x4 -> x7, waiting for transfers between devices: 0.01 us -> 18.7 us  [move(): return lax.ppermute(value, axis, pairs)]
    pallas_call x0 -> x6, Pallas kernels: none -> 18.6 us  [call(): pl.pallas_call(body, out_shape=outs, in_specs=[pl.BlockSpec(memory_space=...]
    dot_general x9 -> x0, matrix products: 14.1 us -> none  [transpose_conv(): jnp.einsum('myxo,mco->yxc', window, flipped[:, row_tap, col_tap], preferr...]
    all_to_all x0 -> x1, starting transfers between devices: none -> 13 us  [swap(): return lax.all_to_all(sums, ('frames', 'rows'), 0, 0, tiled=True)]
    all_to_all x0 -> x1, blocking collectives: none -> 13 us  [swap(): return lax.all_to_all(sums, ('frames', 'rows'), 0, 0, tiled=True)]
    unnamed x34 -> x22, local copies, waits for them, and re-layouts: 0.1 us -> 9.48 us
    slice x10 -> x2, local copies, waits for them, and re-layouts: 9.11 us -> 1.92 us  [the longest x1 1.07 us: shards(): ends = jnp.concatenate([slab[:1], slab[strip - 1:]])]
  transfers between devices with their start and end apart: 4 -> 8, of which waited for: 0 -> 1; matrix products, arithmetic and copies ran while one was open for 14% -> 2% of each run, Pallas kernels for 0% -> 17%
where the time goes in v2:
time: 82.8 us; the launch traced here: 82.3 us
  starting transfers between devices  20.4 us (25%)
  waiting for transfers between devices  18.7 us (23%)
  Pallas kernels  18.6 us (22%)
  blocking collectives  13 us (16%)
  local copies, waits for them, and re-layouts  11.4 us (14%)
    ppermute x7, waiting for transfers between devices, move(): return lax.ppermute(value, axis, pairs)  18.7 us
    pallas_call x6, Pallas kernels, call(): pl.pallas_call(body, out_shape=outs, in_specs=[pl.BlockSpec(memory_space=...  18.6 us
    all_to_all x1, starting transfers between devices, swap(): return lax.all_to_all(sums, ('frames', 'rows'), 0, 0, tiled=True)  13 us
    all_to_all x1, blocking collectives, swap(): return lax.all_to_all(sums, ('frames', 'rows'), 0, 0, tiled=True)  13 us
    unnamed x22, local copies, waits for them, and re-layouts  9.48 us
    ppermute x7, starting transfers between devices, move(): return lax.ppermute(value, axis, pairs)  7.39 us
  transfers between devices with their start and end apart: 8, of which 1 were waited for; matrix products, arithmetic and copies ran while one was open for 2% of the time, Pallas kernels for 17%

profile of v2, /device:TPU:0, one launch (start us, length us, event | category | flops | bytes accessed | tf_op | source)
XLA Modules:
  0.0 82.3 jit_solution(10355829665961223136)
XLA Ops:
  0.0 1.3 %collective-permute-start.1 = (bf16[4,424,256]{2,1,0:T(8,128)(2,1)}, bf16[4,424,256]{2,1,0:T(8,128)(2,1)S(1)}, u32[]{:S(2)}, u32[]{:S(2)}) collective-permute-start(bf16[4,424,256]{2,1,0:T(8,128)(2,1)} %bitcast.7), channel_id=1, source_target_pairs={{16,0},{17,1},{18,2},{19,3},{20,4},{21,5},{22,6},{23,7}} | collective-permute-start | bytes 2605064 | tf_op jit(solution)/shard_map/ppermute | solution.py:220
  1.3 1.3 %collective-permute-start = (bf16[4,424,256]{2,1,0:T(8,128)(2,1)}, bf16[4,424,256]{2,1,0:T(8,128)(2,1)S(1)}, u32[]{:S(2)}, u32[]{:S(2)}) collective-permute-start(bf16[4,424,256]{2,1,0:T(8,128)(2,1)} %bitcast.8), channel_id=1, source_target_pairs={{8,0},{24,16},{9,1},{25,17},{10,2},{26,18},{11,3},{27,19},{12,4},{... | collective-permute-start | bytes 2605064 | tf_op jit(solution)/shard_map/ppermute | solution.py:220
  2.6 0.7 collective-permute-start.3
  3.3 1.1 %slice_bitcast_fusion.1 = (bf16[1,424,256]{2,1,0:T(8,128)(2,1)S(1)}, bf16[1,424,256]{2,1,0:T(8,128)(2,1)S(1)}) fusion(bf16[1,4,424,256]{3,2,1,0:T(8,128)(2,1)} %slab_ref.1), kind=kLoop, calls=%fused_computation.2 | loop fusion | bytes 868352 | tf_op jit(solution)/shard_map/slice | solution.py:228
  4.4 0.7 collective-permute-start.4
  5.1 18.7 %collective-permute-done.1.le_ref = bf16[4,424,256]{2,1,0:T(8,128)(2,1)S(1)} collective-permute-done((bf16[4,424,256]{2,1,0:T(8,128)(2,1)}, bf16[4,424,256]{2,1,0:T(8,128)(2,1)S(1)}, u32[]{:S(2)}, u32[]{:S(2)}) %collective-permute-start.1) | collective-permute-done | bytes 868384 | tf_op jit(solution)/shard_map/ppermute | solution.py:220
  23.8 0.0 copy-start.2
  23.8 0.8 %slice.20 = bf16[2,424,256]{2,1,0:T(8,128)(2,1)} slice(bf16[4,424,256]{2,1,0:T(8,128)(2,1)S(1)} %collective-permute-done.1.le_ref), slice={[1:3], [0:424], [0:256]} | slice | bytes 868352 | tf_op jit(solution)/shard_map/slice | solution.py:230
  24.6 2.0 %collective-permute-start.2 = (bf16[2,424,256]{2,1,0:T(8,128)(2,1)}, bf16[2,424,256]{2,1,0:T(8,128)(2,1)}, u32[]{:S(2)}, u32[]{:S(2)}) collective-permute-start(bf16[2,424,256]{2,1,0:T(8,128)(2,1)} %slice.20), channel_id=1, source_target_pairs={{0,8},{1,9},{2,10},{3,11},{4,12},{5,13},{6,14},{7,15}} | collective-permute-start | bytes 1302536 | tf_op jit(solution)/shard_map/ppermute | solution.py:220
  26.7 3.8 %shard_map.55 = (f32[6,424,256]{2,1,0:T(8,128)S(1)}, bf16[3,3,3,256,256]{4,3,2,1,0:T(8,128)(2,1)S(1)}) custom-call(bf16[1,4,424,256]{3,2,1,0:T(8,128)(2,1)} %slab_ref.1, bf16[3,3,3,256,256]{4,3,2,1,0:T(8,128)(2,1)} %far_ref.1), custom_call_target="tpu_custom_call" | custom-call | flops 2000683008 | bytes 5210112 | tf_op jit(solution)/shard_map/pallas_call | solution.py:20
  30.5 0.0 collective-permute-done.4.dl_ref
  30.6 0.0 collective-permute-done.xl_ref
  30.6 0.0 copy-start.4
  30.6 0.0 collective-permute-done.3.lo_ref
  30.6 0.0 copy-start.6
  30.6 0.0 copy-done.2
  30.6 5.0 %shard_map.56 = (f32[4,424,256]{2,1,0:T(8,128)S(1)}, bf16[424,256]{1,0:T(8,128)(2,1)}, bf16[424,256]{1,0:T(8,128)(2,1)}) custom-call(bf16[4,424,256]{2,1,0:T(8,128)(2,1)S(1)} %collective-permute-done.xl_ref, bf16[2,424,256]{2,1,0:T(8,128)(2,1)S(1)} %collective-permute-done.4.dl_ref, bf16[4,424,256]{2,1,0:T(8,128)(2,1)S(1)} %collective-permute-done.1.le_ref, ...), custom_call_target="tpu_custom_call" | custom-call | flops 2000683008 | bytes 13893632 | tf_op jit(solution)/shard_map/pallas_call | solution.py:20
  35.6 0.0 copy-done.4
  35.7 0.0 copy-done.6
  35.7 0.0 copy-start.8
  35.7 1.2 %copy-done.8 = f32[4,424,256]{2,1,0:T(8,128)} copy-done((f32[4,424,256]{2,1,0:T(8,128)}, f32[4,424,256]{2,1,0:T(8,128)S(1)}, u32[]{:S(2)}) %copy-start.8) | copy-done | bytes 1736728
  36.9 0.0 collective-permute-start.5
  36.9 1.4 %collective-permute-start.6 = (bf16[424,256]{1,0:T(8,128)(2,1)}, bf16[424,256]{1,0:T(8,128)(2,1)}, u32[]{:S(2)}, u32[]{:S(2)}) collective-permute-start(bf16[424,256]{1,0:T(8,128)(2,1)} %get-tuple-element.18), channel_id=1, source_target_pairs={{1,2},{3,4},{5,6},{2,1},{4,3},{6,5},{9,10},{11,12},{13,14},{10,9},... | collective-permute-start | bytes 651272 | tf_op jit(solution)/shard_map/ppermute | solution.py:220
  38.3 1.6 %shard_map.58 = f32[32,2,256]{2,1,0:T(2,128)S(1)} custom-call(bf16[1,4,424,256]{3,2,1,0:T(8,128)(2,1)} %far_x_ref.1), custom_call_target="tpu_custom_call" | custom-call | flops 3473408 | bytes 868352 | tf_op jit(solution)/shard_map/pallas_call | solution.py:20
  39.8 0.0 copy-start.10
  39.9 0.6 copy-done.10
  40.5 13.0 %all-to-all-start = ((f32[32,2,256]{2,1,0:T(2,128)}), f32[32,2,256]{2,1,0:T(2,128)}, u32[]{:S(2)}, u32[]{:S(2)}) async-start(f32[32,2,256]{2,1,0:T(2,128)} %copy-done.10), calls=%async_computation | async-start | bytes 131072 | tf_op jit(solution)/shard_map/all_to_all | solution.py:223
  53.5 0.0 collective-permute-done.2.rl_ref
  53.5 0.0 copy-start.3
  53.5 1.2 %copy-done.3 = bf16[4,424,256]{2,1,0:T(8,128)(2,1)S(1)} copy-done((bf16[4,424,256]{2,1,0:T(8,128)(2,1)S(1)}, bf16[4,424,256]{2,1,0:T(8,128)(2,1)}, u32[]{:S(2)}) %copy-start.3) | copy-done | bytes 868376
  54.6 0.0 copy-start.5
  54.6 1.2 %copy-done.5 = bf16[4,424,256]{2,1,0:T(8,128)(2,1)S(1)} copy-done((bf16[4,424,256]{2,1,0:T(8,128)(2,1)S(1)}, bf16[4,424,256]{2,1,0:T(8,128)(2,1)}, u32[]{:S(2)}) %copy-start.5) | copy-done | bytes 868376
  55.8 0.0 copy-start.7
  55.8 1.2 %copy-done.7 = bf16[4,424,256]{2,1,0:T(8,128)(2,1)S(1)} copy-done((bf16[4,424,256]{2,1,0:T(8,128)(2,1)S(1)}, bf16[4,424,256]{2,1,0:T(8,128)(2,1)}, u32[]{:S(2)}) %copy-start.7) | copy-done | bytes 868376
  57.0 0.0 copy-start.9
  57.0 1.5 %copy-done.9 = f32[4,424,256]{2,1,0:T(8,128)S(1)} copy-done((f32[4,424,256]{2,1,0:T(8,128)S(1)}, f32[4,424,256]{2,1,0:T(8,128)}, u32[]{:S(2)}) %copy-start.9) | copy-done | bytes 1736728
  58.4 3.6 %shard_map.57.acc_ref = f32[4,424,256]{2,1,0:T(8,128)S(1)} custom-call(bf16[4,424,256]{2,1,0:T(8,128)(2,1)S(1)} %copy-done.5, bf16[2,424,256]{2,1,0:T(8,128)(2,1)} %collective-permute-done.2.rl_ref, bf16[4,424,256]{2,1,0:T(8,128)(2,1)S(1)} %copy-done.3, bf16[4,424,256]{2,1,0:T(8,128)(2,1)S(1)} %copy-done.7, ...), custom_call_target="tpu_custom_call" | custom-call | flops 2000683008 | bytes 10420224 | tf_op jit(solution)/shard_map/pallas_call | solution.py:20
  62.0 0.0 copy-start
  62.0 1.2 %copy-done = f32[4,424,256]{2,1,0:T(8,128)} copy-done((f32[4,424,256]{2,1,0:T(8,128)}, f32[4,424,256]{2,1,0:T(8,128)S(1)}, u32[]{:S(2)}) %copy-start) | copy-done | bytes 1736728
  63.2 0.0 all-to-all-done.got_ref
  63.2 0.0 collective-permute-done.5.mate_ref
  63.2 0.0 collective-permute-done.6.other_ref
  63.2 0.0 copy-start.1
  63.3 1.5 %copy-done.1 = f32[4,424,256]{2,1,0:T(8,128)S(1)} copy-done((f32[4,424,256]{2,1,0:T(8,128)S(1)}, f32[4,424,256]{2,1,0:T(8,128)}, u32[]{:S(2)}) %copy-start.1) | copy-done | bytes 1736728
  64.7 3.4 %shard_map.59 = (f32[4,424,256]{2,1,0:T(8,128)S(1)}, bf16[4,424,256]{2,1,0:T(8,128)(2,1)S(1)}, f32[8,256]{1,0:T(8,128)S(1)}, f32[32,2,256]{2,1,0:T(2,128)S(1)}) custom-call(f32[4,424,256]{2,1,0:T(8,128)S(1)} %copy-done.1, bf16[424,256]{1,0:T(8,128)(2,1)} %collective-permute-done.5.mate_ref, bf16[424,256]{1,0:T(8,128)(2,1)} %collective-permute-done.6.other_ref, ...), custom_call_target="tpu_custom_call" | custom-call | flops 17367040 | bytes 3473408 | tf_op jit(solution)/shard_map/pallas_call | solution.py:20
  68.2 13.0 %all_to_all.10.sums_ref = f32[32,2,256]{2,1,0:T(2,128)S(1)} all-to-all(f32[32,2,256]{2,1,0:T(2,128)S(1)} %get-tuple-element.22), channel_id=1, replica_groups=mesh['frames'=4,'rows'=8] {'frames','rows'}, dimensions={0} | all-to-all | bytes 131072 | tf_op jit(solution)/shard_map/all_to_all | solution.py:223
  81.1 1.2 %shard_map.60 = bf16[1,4,424,256]{3,2,1,0:T(8,128)(2,1)} custom-call(f32[4,424,256]{2,1,0:T(8,128)S(1)} %get-tuple-element.19.grad_ref, bf16[4,424,256]{2,1,0:T(8,128)(2,1)S(1)} %get-tuple-element.20.x_ref, f32[8,256]{1,0:T(8,128)S(1)} %get-tuple-element.21.params_ref, f32[32,2,256]{2,1,0:T(2,128)S(1)} %all_to_all.10.sums_ref), custom_call_target="tpu_custom_call" | custom-call | flops 4341760 | bytes 3473408 | tf_op jit(solution)/shard_map/pallas_call | solution.py:20
  (1 shorter events, 0.0 us)
Async XLA Ops:
  0.0 23.8 %collective-permute-start.1 = (bf16[4,424,256]{2,1,0:T(8,128)(2,1)}, bf16[4,424,256]{2,1,0:T(8,128)(2,1)S(1)}, u32[]{:S(2)}, u32[]{:S(2)}) collective-permute-start(bf16[4,424,256]{2,1,0:T(8,128)(2,1)} %bitcast.7), channel_id=1, source_target_pairs={{16,0},{17,1},{18,2},{19,3},{20,4},{21,5},{22,6},{23,7}} | collective-permute-start | bytes 2605064 | tf_op jit(solution)/shard_map/ppermute | solution.py:220
  1.3 29.3 %collective-permute-start = (bf16[4,424,256]{2,1,0:T(8,128)(2,1)}, bf16[4,424,256]{2,1,0:T(8,128)(2,1)S(1)}, u32[]{:S(2)}, u32[]{:S(2)}) collective-permute-start(bf16[4,424,256]{2,1,0:T(8,128)(2,1)} %bitcast.8), channel_id=1, source_target_pairs={{8,0},{24,16},{9,1},{25,17},{10,2},{26,18},{11,3},{27,19},{12,4},{... | collective-permute-start | bytes 2605064 | tf_op jit(solution)/shard_map/ppermute | solution.py:220
  2.6 28.0 %collective-permute-start.3 = (bf16[4,424,256]{2,1,0:T(8,128)(2,1)}, bf16[4,424,256]{2,1,0:T(8,128)(2,1)S(1)}, u32[]{:S(2)}, u32[]{:S(2)}) collective-permute-start(bf16[4,424,256]{2,1,0:T(8,128)(2,1)} %bitcast.9), channel_id=1, source_target_pairs={{24,8},{25,9},{26,10},{27,11},{28,12},{29,13},{30,14},{31,15}} | collective-permute-start | bytes 2605064 | tf_op jit(solution)/shard_map/ppermute | solution.py:220
  4.4 26.1 %collective-permute-start.4 = (bf16[2,424,256]{2,1,0:T(8,128)(2,1)S(1)}, bf16[2,424,256]{2,1,0:T(8,128)(2,1)S(1)}, u32[]{:S(2)}, u32[]{:S(2)}) collective-permute-start(bf16[2,424,256]{2,1,0:T(8,128)(2,1)S(1)} %pad_maximum_fusion), channel_id=1, source_target_pairs={{16,8},{17,9},{18,10},{19,11},{20,12},{21,13},{22,14},{23,15}} | collective-permute-start | bytes 1302536 | tf_op jit(solution)/shard_map/ppermute | solution.py:220
  23.8 6.8 %copy-start.2 = (bf16[4,424,256]{2,1,0:T(8,128)(2,1)}, bf16[4,424,256]{2,1,0:T(8,128)(2,1)S(1)}, u32[]{:S(2)}) copy-start(bf16[4,424,256]{2,1,0:T(8,128)(2,1)S(1)} %collective-permute-done.1.le_ref) | copy-start | bytes 2605060
  24.6 28.8 %collective-permute-start.2 = (bf16[2,424,256]{2,1,0:T(8,128)(2,1)}, bf16[2,424,256]{2,1,0:T(8,128)(2,1)}, u32[]{:S(2)}, u32[]{:S(2)}) collective-permute-start(bf16[2,424,256]{2,1,0:T(8,128)(2,1)} %slice.20), channel_id=1, source_target_pairs={{0,8},{1,9},{2,10},{3,11},{4,12},{5,13},{6,14},{7,15}} | collective-permute-start | bytes 1302536 | tf_op jit(solution)/shard_map/ppermute | solution.py:220
  30.6 5.1 %copy-start.4 = (bf16[4,424,256]{2,1,0:T(8,128)(2,1)}, bf16[4,424,256]{2,1,0:T(8,128)(2,1)S(1)}, u32[]{:S(2)}) copy-start(bf16[4,424,256]{2,1,0:T(8,128)(2,1)S(1)} %collective-permute-done.xl_ref) | copy-start | bytes 2605060
  30.6 5.1 %copy-start.6 = (bf16[4,424,256]{2,1,0:T(8,128)(2,1)}, bf16[4,424,256]{2,1,0:T(8,128)(2,1)S(1)}, u32[]{:S(2)}) copy-start(bf16[4,424,256]{2,1,0:T(8,128)(2,1)S(1)} %collective-permute-done.3.lo_ref) | copy-start | bytes 2605060
  35.7 1.2 %copy-start.8 = (f32[4,424,256]{2,1,0:T(8,128)}, f32[4,424,256]{2,1,0:T(8,128)S(1)}, u32[]{:S(2)}) copy-start(f32[4,424,256]{2,1,0:T(8,128)S(1)} %get-tuple-element.16.acc_ref) | copy-start | bytes 5210116
  36.9 26.3 %collective-permute-start.5 = (bf16[424,256]{1,0:T(8,128)(2,1)}, bf16[424,256]{1,0:T(8,128)(2,1)}, u32[]{:S(2)}, u32[]{:S(2)}) collective-permute-start(bf16[424,256]{1,0:T(8,128)(2,1)} %get-tuple-element.17), channel_id=1, source_target_pairs={{0,1},{1,0},{2,3},{3,2},{4,5},{5,4},{6,7},{7,6},{8,9},{9,8},{10,11... | collective-permute-start | bytes 651272 | tf_op jit(solution)/shard_map/ppermute | solution.py:220
  36.9 26.3 %collective-permute-start.6 = (bf16[424,256]{1,0:T(8,128)(2,1)}, bf16[424,256]{1,0:T(8,128)(2,1)}, u32[]{:S(2)}, u32[]{:S(2)}) collective-permute-start(bf16[424,256]{1,0:T(8,128)(2,1)} %get-tuple-element.18), channel_id=1, source_target_pairs={{1,2},{3,4},{5,6},{2,1},{4,3},{6,5},{9,10},{11,12},{13,14},{10,9},... | collective-permute-start | bytes 651272 | tf_op jit(solution)/shard_map/ppermute | solution.py:220
  39.8 0.6 copy-start.10
  40.5 22.8 %all-to-all-start = ((f32[32,2,256]{2,1,0:T(2,128)}), f32[32,2,256]{2,1,0:T(2,128)}, u32[]{:S(2)}, u32[]{:S(2)}) async-start(f32[32,2,256]{2,1,0:T(2,128)} %copy-done.10), calls=%async_computation | async-start | bytes 131072 | tf_op jit(solution)/shard_map/all_to_all | solution.py:223
  53.5 1.2 %copy-start.3 = (bf16[4,424,256]{2,1,0:T(8,128)(2,1)S(1)}, bf16[4,424,256]{2,1,0:T(8,128)(2,1)}, u32[]{:S(2)}) copy-start(bf16[4,424,256]{2,1,0:T(8,128)(2,1)} %copy-done.2) | copy-start | bytes 2605060
  54.6 1.2 %copy-start.5 = (bf16[4,424,256]{2,1,0:T(8,128)(2,1)S(1)}, bf16[4,424,256]{2,1,0:T(8,128)(2,1)}, u32[]{:S(2)}) copy-start(bf16[4,424,256]{2,1,0:T(8,128)(2,1)} %copy-done.4) | copy-start | bytes 2605060
  55.8 1.2 %copy-start.7 = (bf16[4,424,256]{2,1,0:T(8,128)(2,1)S(1)}, bf16[4,424,256]{2,1,0:T(8,128)(2,1)}, u32[]{:S(2)}) copy-start(bf16[4,424,256]{2,1,0:T(8,128)(2,1)} %copy-done.6) | copy-start | bytes 2605060
  57.0 1.5 %copy-start.9 = (f32[4,424,256]{2,1,0:T(8,128)S(1)}, f32[4,424,256]{2,1,0:T(8,128)}, u32[]{:S(2)}) copy-start(f32[4,424,256]{2,1,0:T(8,128)} %copy-done.8) | copy-start | bytes 5210116
  62.0 1.2 %copy-start = (f32[4,424,256]{2,1,0:T(8,128)}, f32[4,424,256]{2,1,0:T(8,128)S(1)}, u32[]{:S(2)}) copy-start(f32[4,424,256]{2,1,0:T(8,128)S(1)} %shard_map.57.acc_ref) | copy-start | bytes 5210116
  63.2 1.5 %copy-start.1 = (f32[4,424,256]{2,1,0:T(8,128)S(1)}, f32[4,424,256]{2,1,0:T(8,128)}, u32[]{:S(2)}) copy-start(f32[4,424,256]{2,1,0:T(8,128)} %copy-done) | copy-start | bytes 5210116

commit v3 on v2

v3 whole, which is shorter than its diff:
```python
import functools
import jax
import jax.numpy as jnp
from jax import lax
from jax.experimental import pallas as pl
from jax.experimental.pallas import tpu as pltpu
from jax.sharding import PartitionSpec as P

GROUPS = 32
EPS = 1e-06
F32 = jnp.float32
BF16 = jnp.bfloat16
HIGH = lax.Precision.HIGHEST
DMA = pltpu.SemaphoreType.DMA
LIMIT = 24 * 1024 * 1024


def call(body, outs, flops, moved, args, near=(), far=(), scratch=()):
    spaces = [pltpu.VMEM if n in near else pltpu.HBM if n in far else None for n in range(len(args))]
    return pl.pallas_call(
        body,
        out_shape=outs,
        in_specs=[pl.BlockSpec(memory_space=m or pl.ANY) for m in spaces],
        out_specs=[
            pl.BlockSpec(memory_space=getattr(o, "memory_space", pltpu.HBM))
            for o in outs
        ],
        scratch_shapes=list(scratch),
        cost_estimate=pl.CostEstimate(flops=flops, bytes_accessed=moved, transcendentals=0),
        compiler_params=pltpu.CompilerParams(vmem_limit_bytes=LIMIT),
    )(*(v if m is None else pltpu.with_memory_space_constraint(v, m) for v, m in zip(args, spaces)))


def fetch(sems, *pairs):
    copies = [pltpu.make_async_copy(a, b, sems.at[n]) for n, (a, b) in enumerate(pairs)]
    for copy in copies:
        copy.start()
    return copies


def same_group(channels):
    per = channels // GROUPS
    one = lax.broadcasted_iota(jnp.int32, (channels, channels), 0) // per
    two = lax.broadcasted_iota(jnp.int32, (channels, channels), 1) // per
    return (one == two).astype(F32)


def pack_sums(first, second, out_ref):
    channels = first.shape[-1]
    row = lax.broadcasted_iota(jnp.int32, (8, channels), 0)
    both = jnp.where(row == 0, first, jnp.where(row == 1, second, 0.0))
    sums = jnp.dot(both, same_group(channels), precision=HIGH, preferred_element_type=F32)
    out_ref[...] = jnp.broadcast_to(sums[None, 0:2], out_ref.shape)


def cut_body(slab_ref, inner_ref, ends_ref, sems):
    strip = slab_ref.shape[1]
    for copy in fetch(
        sems, (slab_ref.at[0, 0], ends_ref.at[0]), (slab_ref.at[0, strip - 1], ends_ref.at[1]),
        (slab_ref.at[0, 1 : strip - 1], inner_ref),
    ):
        copy.wait()


def stats_body(x_ref, out_ref, near, sems):
    _, strip, _, c = x_ref.shape
    copies = fetch(sems, *((x_ref.at[0, y], near.at[y]) for y in range(strip)))
    first, second = jnp.zeros((1, c), F32), jnp.zeros((1, c), F32)
    for y in range(strip):
        copies[y].wait()
        v = near[y].astype(F32)
        first = first + jnp.sum(v, axis=0, keepdims=True)
        second = second + jnp.sum(v * v, axis=0, keepdims=True)
    pack_sums(first, second, out_ref)


def taps(lhs, w):
    return lax.dot_general(lhs, w, (((1,), (1,)), ((), ())), preferred_element_type=F32)


def columns(a):
    width, wide = a.shape
    c = wide // 3
    at = lax.broadcasted_iota(jnp.int32, (8, c), 0)
    left = pltpu.roll(a[:, :c], width - 1, 0)
    right = pltpu.roll(a[:, 2 * c :], 1, 0)
    left = jnp.concatenate([left[: width - 8], jnp.where(at == 7, 0.0, left[width - 8 :])], axis=0)
    right = jnp.concatenate([jnp.where(at == 0, 0.0, right[:8]), right[8:]], axis=0)
    return a[:, c : 2 * c] + left + right


def flat(w_ref, frame_tap, row_tap):
    c = w_ref.shape[-1]
    return w_ref[frame_tap, row_tap].reshape(3 * c, c)


def own_body(
    slab_ref, far_ref, gain_ref, bias_ref, acc_ref, gains_ref, biases_ref, slab, w_own, rows, sems, out_sems
):
    _, strip, _, c = slab_ref.shape
    copies = fetch(
        sems, (slab_ref.at[0], slab), (far_ref.at[2], w_own), (gain_ref, gains_ref), (bias_ref, biases_ref)
    )
    copies[0].wait()
    copies[1].wait()
    leaving = []
    for y in range(-1, strip + 1):
        use = [(y + 1 - i, i) for i in range(3) if 0 <= y + 1 - i < strip]
        lhs = jnp.concatenate([slab[r] for r, _ in use], axis=1)
        w = jnp.concatenate([w_own[i].reshape(3 * c, c) for _, i in use], axis=1)
        rows[y + 1] = columns(taps(lhs, w))
        leaving.append(pltpu.make_async_copy(rows.at[y + 1], acc_ref.at[y + 1], out_sems.at[y + 1]))
        leaving[-1].start()
    for copy in copies[2:] + leaving:
        copy.wait()


def load_body(far_ref, w_ref, sems):
    for copy in fetch(sems, *((far_ref.at[k], w_ref.at[k]) for k in range(2))):
        copy.wait()


def either(mine, start_odd, start_even):
    @pl.when(mine)
    def _():
        for copy in start_odd:
            copy.start()

    @pl.when(jnp.logical_not(mine))
    def _():
        for copy in start_even:
            copy.start()


def fetch_ends(side_ref, dl_ref, later, sems):
    top = side_ref.shape[0] - 1
    copy = pltpu.make_async_copy
    of_odd = [copy(dl_ref.at[n], later.at[n], sems.at[n]) for n in range(2)]
    of_even = [copy(side_ref.at[n * top], later.at[n], sems.at[n]) for n in range(2)]
    either(lax.axis_index("frames") % 2 == 1, of_odd, of_even)
    return of_odd


def edge_body(
    side_ref, dl_ref, le_ref, w_ref, acc_ref, mate_ref, other_ref, later_ref, latest_ref, leave, edges, sems
):
    strip = side_ref.shape[0]
    odd_line = lax.axis_index("rows") % 2
    of_odd = fetch_ends(side_ref, dl_ref, later_ref, sems)
    rest = fetch(
        sems.at[2:6], *((le_ref.at[n], latest_ref.at[n]) for n in range(2)),
        *((acc_ref.at[n * (strip + 1)], edges.at[n]) for n in range(2)),
    )
    for n in range(2):
        for one in (of_odd[n], rest[n], rest[2 + n]):
            one.wait()
        lhs = jnp.concatenate([later_ref[n], latest_ref[n]], axis=1)
        w = jnp.concatenate([flat(w_ref, 1, 2 * n), flat(w_ref, 0, 2 * n)], axis=1)
        leave[n] = (edges[n] + columns(taps(lhs, w))).astype(BF16)
    mate_ref[...] = leave[1 - odd_line]
    other_ref[...] = leave[odd_line]


def mid_body(
    cells, side_ref, dl_ref, le_ref, w_ref, far_acc_ref, far_x_ref, gains_ref, biases_ref, got_ref,
    acc_ref, factor_ref, x_ref, params_ref, later_ref, latest_ref, got, sems,
):
    strip = acc_ref.shape[0]
    top = strip - 1
    copies = fetch(
        sems.at[2 : 5 + strip], (got_ref, got), *((far_x_ref.at[0, y], x_ref.at[y]) for y in range(strip)),
        (far_acc_ref.at[1 : strip + 1], acc_ref), (le_ref, latest_ref),
    )
    copies += fetch_ends(side_ref, dl_ref, later_ref, sems)
    copies[0].wait()
    total = jnp.sum(got[...], axis=0) / cells
    centre = total[0:1]
    variance = jnp.maximum(total[1:2] - centre * centre, 0.0)
    inv_std = lax.rsqrt(variance + EPS)
    params_ref[0:1] = centre
    params_ref[1:2] = inv_std
    gain, bias = gains_ref[...], biases_ref[...]
    scale = inv_std * gain
    for copy in copies[1:]:
        copy.wait()
    for n, r in enumerate((0, top)):
        lhs = jnp.concatenate([later_ref[n], latest_ref[n]], axis=1)
        for i in range(3):
            y = r - 1 + i
            if 0 <= y < strip:
                w = jnp.concatenate([flat(w_ref, 1, i), flat(w_ref, 0, i)], axis=1)
                acc_ref[y] += columns(taps(lhs, w))
                preact = (x_ref[y].astype(F32) - centre) * scale + bias
                logistic = 0.5 + 0.5 * jnp.tanh(0.5 * preact)
                factor_ref[y] = logistic * (1.0 + preact * (1.0 - logistic)) * gain


def rest_body(
    side_ref, r1_ref, e1_ref, oi_ref, w_ref, acc_ref, factor_ref, x_ref, params_ref, mate_ref, other_ref,
    grad_ref, sums_ref, later, latest, mate, other, sems,
):
    strip, _, c = acc_ref.shape
    top = strip - 1
    odd_frame, odd_line = lax.axis_index("frames") % 2 == 1, lax.axis_index("rows") % 2
    copy = pltpu.make_async_copy
    of_odd = [copy(r1_ref, later, sems.at[0]), copy(oi_ref, latest, sems.at[1])]
    of_even = [copy(side_ref.at[1:top], later, sems.at[0]), copy(e1_ref, latest, sems.at[1])]
    either(odd_frame, of_odd, of_even)
    for one in of_odd + fetch(sems.at[2:4], (mate_ref, mate), (other_ref, other)):
        one.wait()
    centre, inv_std = params_ref[0:1], params_ref[1:2]
    frames = [jnp.concatenate([later[r], latest[r]], axis=1) for r in range(strip - 2)]
    first, second = jnp.zeros((1, c), F32), jnp.zeros((1, c), F32)
    for y in range(strip):
        use = [(y + 1 - i, i) for i in range(3) if 1 <= y + 1 - i < top]
        lhs = jnp.concatenate([frames[r - 1] for r, _ in use], axis=1)
        w = jnp.concatenate([flat(w_ref, k, i) for _, i in use for k in (1, 0)], axis=1)
        value = acc_ref[y] + columns(taps(lhs, w))
        if y in (0, top):
            from_mate = odd_line == (1 if y == 0 else 0)
            value = value + jnp.where(from_mate, mate[...].astype(F32), other[...].astype(F32))
        grad = value * factor_ref[y]
        grad_ref[y] = grad
        first = first + jnp.sum(grad, axis=0, keepdims=True)
        second = second + jnp.sum(grad * (x_ref[y].astype(F32) - centre), axis=0, keepdims=True)
    pack_sums(first, second * inv_std, sums_ref)


def final_body(cells, grad_ref, x_ref, params_ref, sums_ref, out_ref, rows, sems):
    strip = x_ref.shape[0]
    centre, inv_std = params_ref[0:1], params_ref[1:2]
    means = jnp.sum(sums_ref[...], axis=0) / cells
    total, cross = means[0:1], means[1:2]
    copies = []
    for y in range(strip):
        normed = (x_ref[y].astype(F32) - centre) * inv_std
        rows[y] = (inv_std * (grad_ref[y] - total - normed * cross)).astype(BF16)
        copies.append(pltpu.make_async_copy(rows.at[y], out_ref.at[0, y], sems.at[y]))
        copies[-1].start()
    for copy in copies:
        copy.wait()


def shards(inputs, cotangent, kernel, norm_gain, norm_bias):
    _, strip, width, c = inputs.shape
    frames, lines = lax.axis_size("frames"), lax.axis_size("rows")
    devices = frames * lines
    cells = float(devices * strip * width * (c // GROUPS))
    size = width * c
    tap = 2 * size * c * 3
    whole, pair, line = (strip, width, c), (strip - 2, width, c), (width, c)
    near = lambda shape, kind=F32: pltpu.VMEM(shape, kind)
    sums_shape = near((devices, 2, c))
    slab = cotangent[0]

    def move(value, pairs, axis="frames"):
        return lax.ppermute(value, axis, pairs)

    def swap(sums):
        return lax.all_to_all(sums, ("frames", "rows"), 0, 0, tiled=True)

    inner, ends = call(
        cut_body, [near(pair, BF16), near((2, width, c), BF16)], 0, 4 * strip * size, (cotangent,), far=(0,),
        scratch=[DMA((3,))],
    )
    evens = [(i, i - 1) for i in range(2, frames, 2)]
    direct = move(ends, evens)
    e1 = move(inner, [(i, i - 2) for i in range(2, frames, 2)])
    latest_ends = move(ends, [(i, i - 2) for i in range(2, frames)])
    later_x = move(slab, [(i, i - 1) for i in range(1, frames, 2)])
    odd_inner = move(inner, [(i, i - 2) for i in range(3, frames, 2)])
    r1 = move(e1, [(i, i + 1) for i in range(0, frames - 2, 2)])

    (sums,) = call(
        stats_body, [sums_shape], 8 * strip * size, 2 * strip * size, (inputs,), far=(0,),
        scratch=[near(whole, BF16), DMA((strip,))],
    )
    got = swap(sums)
    vec, two, row8 = near((1, c)), near((2, width, c), BF16), near((8, c))
    acc, gains, biases = call(
        own_body, [pltpu.HBM((strip + 2, width, c), F32), vec, vec],
        tap * 3 * strip, 8 * 6 * size, (cotangent, kernel, norm_gain.reshape(1, c), norm_bias.reshape(1, c)),
        far=(0, 1, 2, 3),
        scratch=[near(whole, BF16), near(kernel.shape[1:], BF16), near((strip + 2, width, c)), DMA((4,)),
                 DMA((strip + 2,))],
    )
    (w,) = call(
        load_body, [near((2,) + kernel.shape[1:], BF16)], 0, 4 * 18 * c * c, (kernel,), far=(0,),
        scratch=[DMA((2,))],
    )
    mate, other = call(
        edge_body, [near(line, BF16), near(line, BF16)], tap * 4, 8 * 8 * size,
        (later_x, direct, latest_ends, w, acc), near=(3,), far=(4,),
        scratch=[two, two, two, near((2, width, c)), DMA((6,))],
    )
    mate = move(mate, [(i, i ^ 1) for i in range(lines)], "rows")
    between = [(i, i + 1) for i in range(1, lines - 1, 2)]
    other = move(other, between + [(j, i) for i, j in between], "rows")
    acc, factor, x, params = call(
        functools.partial(mid_body, cells), [near(whole), near(whole), near(whole, BF16), row8],
        tap * 8, 8 * 10 * size,
        (later_x, direct, latest_ends, w, acc, inputs, gains, biases, got), near=(3, 6, 7), far=(4, 5),
        scratch=[two, two, near((devices, 2, c)), DMA((5 + strip,))],
    )
    grad, sums = call(
        rest_body, [near(whole), sums_shape], tap * 12, 8 * 12 * size,
        (later_x, r1, e1, odd_inner, w, acc, factor, x, params, mate, other), near=(4, 5, 6, 7, 8),
        scratch=[near(pair, BF16), near(pair, BF16), near(line, BF16), near(line, BF16), DMA((4,))],
    )
    sums = swap(sums)
    (out,) = call(
        functools.partial(final_body, cells), [jax.ShapeDtypeStruct(inputs.shape, BF16)],
        10 * strip * size, 8 * strip * size, (grad, x, params, sums), near=(0, 1, 2, 3),
        scratch=[near(whole, BF16), DMA((strip,))],
    )
    return out


def solution(mesh):
    return jax.shard_map(
        shards,
        mesh=mesh,
        in_specs=(P("frames", "rows", None, None), P("frames", "rows", None, None), P(), P(), P()),
        out_specs=P("frames", "rows", None, None),
        check_vma=False,
    )
```

time: 82.8 us -> 64.1 us (0.77)
  waiting for transfers between devices: 18.7 us -> 0.02 us
  local copies, waits for them, and re-layouts: 11.4 us -> 0 us
  Pallas kernels: 18.6 us -> 25 us
  starting transfers between devices: 20.4 us -> 23.8 us
  blocking collectives: 13 us -> 14.7 us
    ppermute x7 -> x8, waiting for transfers between devices: 18.7 us -> 0.02 us  [move(): return lax.ppermute(value, axis, pairs)]
    unnamed x22 -> x0, local copies, waits for them, and re-layouts: 9.48 us -> none
    pallas_call x6 -> x8, Pallas kernels: 18.6 us -> 25 us  [call(): pl.pallas_call(body, out_shape=outs, in_specs=[pl.BlockSpec(memory_space=...]
    ppermute x7 -> x8, starting transfers between devices: 7.39 us -> 12.6 us  [move(): return lax.ppermute(value, axis, pairs)]
    slice x2 -> x0, local copies, waits for them, and re-layouts: 1.92 us -> none  [the longest x1 1.07 us: shards(): ends = jnp.concatenate([slab[:1], slab[strip - 1:]])]
    all_to_all x1, starting transfers between devices: 13 us -> 11.2 us  [swap(): return lax.all_to_all(sums, ('frames', 'rows'), 0, 0, tiled=True)]
    all_to_all x1, blocking collectives: 13 us -> 14.7 us  [swap(): return lax.all_to_all(sums, ('frames', 'rows'), 0, 0, tiled=True)]
  transfers between devices with their start and end apart: 8 -> 9, of which waited for: 1 -> 0; matrix products, arithmetic and copies ran while one was open for 2% -> 0% of each run, Pallas kernels for 17% -> 30%
where the time goes in v3:
time: 64.1 us; the launch traced here: 63.7 us
  Pallas kernels  25 us (39%)
  starting transfers between devices  23.8 us (37%)
  blocking collectives  14.7 us (23%)
    pallas_call x8, Pallas kernels, call(): pl.pallas_call(body, out_shape=outs, in_specs=[pl.BlockSpec(memory_space=...  25 us
    all_to_all x1, blocking collectives, swap(): return lax.all_to_all(sums, ('frames', 'rows'), 0, 0, tiled=True)  14.7 us
    ppermute x8, starting transfers between devices, move(): return lax.ppermute(value, axis, pairs)  12.6 us
    all_to_all x1, starting transfers between devices, swap(): return lax.all_to_all(sums, ('frames', 'rows'), 0, 0, tiled=True)  11.2 us
  transfers between devices with their start and end apart: 9, of which 0 were waited for; matrix products, arithmetic and copies ran while one was open for 0% of the time, Pallas kernels for 30%

profile of v3, /device:TPU:0, one launch (start us, length us, event | category | flops | bytes accessed | tf_op | source)
XLA Modules:
  0.0 63.7 jit_solution(17308214740400649266)
XLA Ops:
  0.0 1.3 %collective-permute-start = (bf16[4,424,256]{2,1,0:T(8,128)(2,1)}, bf16[4,424,256]{2,1,0:T(8,128)(2,1)S(1)}, u32[]{:S(2)}, u32[]{:S(2)}) collective-permute-start(bf16[4,424,256]{2,1,0:T(8,128)(2,1)} %bitcast.3), channel_id=1, source_target_pairs={{8,0},{24,16},{9,1},{25,17},{10,2},{26,18},{11,3},{27,19},{12,4},{... | collective-permute-start | bytes 2605064 | tf_op jit(solution)/shard_map/ppermute | solution.py:257
  1.3 2.2 %shard_map.55 = (bf16[2,424,256]{2,1,0:T(8,128)(2,1)}, bf16[2,424,256]{2,1,0:T(8,128)(2,1)}) custom-call(bf16[1,4,424,256]{3,2,1,0:T(8,128)(2,1)} %slab_ref.3), custom_call_target="tpu_custom_call" | custom-call | bytes 1736704 | tf_op jit(solution)/shard_map/pallas_call | solution.py:20
  3.5 1.3 %collective-permute-start.1 = (bf16[2,424,256]{2,1,0:T(8,128)(2,1)}, bf16[2,424,256]{2,1,0:T(8,128)(2,1)}, u32[]{:S(2)}, u32[]{:S(2)}) collective-permute-start(bf16[2,424,256]{2,1,0:T(8,128)(2,1)} %get-tuple-element.18), channel_id=1, source_target_pairs={{16,0},{17,1},{18,2},{19,3},{20,4},{21,5},{22,6},{23,7}} | collective-permute-start | bytes 1302536 | tf_op jit(solution)/shard_map/ppermute | solution.py:257
  4.8 1.4 %collective-permute-start.4 = (bf16[2,424,256]{2,1,0:T(8,128)(2,1)}, bf16[2,424,256]{2,1,0:T(8,128)(2,1)}, u32[]{:S(2)}, u32[]{:S(2)}) collective-permute-start(bf16[2,424,256]{2,1,0:T(8,128)(2,1)} %get-tuple-element.19), channel_id=1, source_target_pairs={{16,8},{17,9},{18,10},{19,11},{20,12},{21,13},{22,14},{23,15}} | collective-permute-start | bytes 1302536 | tf_op jit(solution)/shard_map/ppermute | solution.py:257
  6.2 1.3 %collective-permute-start.5 = (bf16[2,424,256]{2,1,0:T(8,128)(2,1)}, bf16[2,424,256]{2,1,0:T(8,128)(2,1)}, u32[]{:S(2)}, u32[]{:S(2)}) collective-permute-start(bf16[2,424,256]{2,1,0:T(8,128)(2,1)} %get-tuple-element.19), channel_id=1, source_target_pairs={{16,0},{24,8},{17,1},{25,9},{18,2},{26,10},{19,3},{27,11},{20,4},{... | collective-permute-start | bytes 1302536 | tf_op jit(solution)/shard_map/ppermute | solution.py:257
  7.5 1.4 %collective-permute-start.3 = (bf16[2,424,256]{2,1,0:T(8,128)(2,1)}, bf16[2,424,256]{2,1,0:T(8,128)(2,1)}, u32[]{:S(2)}, u32[]{:S(2)}) collective-permute-start(bf16[2,424,256]{2,1,0:T(8,128)(2,1)} %get-tuple-element.18), channel_id=1, source_target_pairs={{24,8},{25,9},{26,10},{27,11},{28,12},{29,13},{30,14},{31,15}} | collective-permute-start | bytes 1302536 | tf_op jit(solution)/shard_map/ppermute | solution.py:257
  8.9 2.2 %shard_map.58 = f32[32,2,256]{2,1,0:T(2,128)} custom-call(bf16[1,4,424,256]{3,2,1,0:T(8,128)(2,1)} %far_x_ref.1), custom_call_target="tpu_custom_call" | custom-call | flops 3473408 | bytes 868352 | tf_op jit(solution)/shard_map/pallas_call | solution.py:20
  11.1 11.2 %all-to-all-start = ((f32[32,2,256]{2,1,0:T(2,128)}), f32[32,2,256]{2,1,0:T(2,128)S(1)}, u32[]{:S(2)}, u32[]{:S(2)}) async-start(f32[32,2,256]{2,1,0:T(2,128)} %shard_map.58), calls=%async_computation | async-start | bytes 131072 | tf_op jit(solution)/shard_map/all_to_all | solution.py:260
  22.3 1.6 %shard_map.56.w_ref = bf16[2,3,3,256,256]{4,3,2,1,0:T(8,128)(2,1)S(1)} custom-call(bf16[3,3,3,256,256]{4,3,2,1,0:T(8,128)(2,1)} %far_ref.3), custom_call_target="tpu_custom_call" | custom-call | bytes 4718592 | tf_op jit(solution)/shard_map/pallas_call | solution.py:20
  24.0 0.0 collective-permute-done.1.e1_ref
  24.0 4.5 %collective-permute-start.2 = (bf16[2,424,256]{2,1,0:T(8,128)(2,1)}, bf16[2,424,256]{2,1,0:T(8,128)(2,1)}, u32[]{:S(2)}, u32[]{:S(2)}) collective-permute-start(bf16[2,424,256]{2,1,0:T(8,128)(2,1)} %collective-permute-done.1.e1_ref), channel_id=1, source_target_pairs={{0,8},{1,9},{2,10},{3,11},{4,12},{5,13},{6,14},{7,15}} | collective-permute-start | bytes 1302536 | tf_op jit(solution)/shard_map/ppermute | solution.py:257
  28.4 4.7 %shard_map.57 = (f32[6,424,256]{2,1,0:T(8,128)}, f32[1,256]{1,0:T(1,128)S(1)}, f32[1,256]{1,0:T(1,128)S(1)}) custom-call(bf16[1,4,424,256]{3,2,1,0:T(8,128)(2,1)} %slab_ref.3, bf16[3,3,3,256,256]{4,3,2,1,0:T(8,128)(2,1)} %far_ref.3, f32[1,256]{1,0:T(1,128)} %bitcast.4, f32[1,256]{1,0:T(1,128)} %bitcast.5), custom_call_target="tpu_custom_call" | custom-call | flops 2000683008 | bytes 5210112 | tf_op jit(solution)/shard_map/pallas_call | solution.py:20
  33.1 0.0 collective-permute-done.4.dl_ref
  33.1 0.0 collective-permute-done.5.le_ref
  33.2 0.0 collective-permute-done.side_ref
  33.2 4.1 %shard_map.60 = (bf16[424,256]{1,0:T(8,128)(2,1)}, bf16[424,256]{1,0:T(8,128)(2,1)}) custom-call(bf16[4,424,256]{2,1,0:T(8,128)(2,1)S(1)} %collective-permute-done.side_ref, bf16[2,424,256]{2,1,0:T(8,128)(2,1)} %collective-permute-done.4.dl_ref, bf16[2,424,256]{2,1,0:T(8,128)(2,1)} %collective-permute-done.5.le_ref, ...), custom_call_target="tpu_custom_call" | custom-call | flops 666894336 | bytes 6946816 | tf_op jit(solution)/shard_map/pallas_call | solution.py:20
  37.2 0.1 collective-permute-start.6
  37.3 1.4 %collective-permute-start.7 = (bf16[424,256]{1,0:T(8,128)(2,1)}, bf16[424,256]{1,0:T(8,128)(2,1)}, u32[]{:S(2)}, u32[]{:S(2)}) collective-permute-start(bf16[424,256]{1,0:T(8,128)(2,1)} %get-tuple-element.28), channel_id=1, source_target_pairs={{1,2},{3,4},{5,6},{2,1},{4,3},{6,5},{9,10},{11,12},{13,14},{10,9},... | collective-permute-start | bytes 651272 | tf_op jit(solution)/shard_map/ppermute | solution.py:257
  38.7 0.0 all-to-all-done.got_ref
  38.7 4.5 %shard_map.59 = (f32[4,424,256]{2,1,0:T(8,128)S(1)}, f32[4,424,256]{2,1,0:T(8,128)S(1)}, bf16[4,424,256]{2,1,0:T(8,128)(2,1)S(1)}, f32[8,256]{1,0:T(8,128)S(1)}) custom-call(bf16[4,424,256]{2,1,0:T(8,128)(2,1)S(1)} %collective-permute-done.side_ref, bf16[2,424,256]{2,1,0:T(8,128)(2,1)} %collective-permute-done.4.dl_ref, ...), custom_call_target="tpu_custom_call" | custom-call | flops 1333788672 | bytes 8683520 | tf_op jit(solution)/shard_map/pallas_call | solution.py:20
  43.2 0.0 collective-permute-done.3.oi_ref
  43.2 0.0 collective-permute-done.2.r1_ref
  43.2 0.0 collective-permute-done.6.mate_ref
  43.2 0.0 collective-permute-done.7.other_ref
  43.2 4.6 %shard_map.61 = (f32[4,424,256]{2,1,0:T(8,128)S(1)}, f32[32,2,256]{2,1,0:T(2,128)S(1)}) custom-call(bf16[4,424,256]{2,1,0:T(8,128)(2,1)S(1)} %collective-permute-done.side_ref, bf16[2,424,256]{2,1,0:T(8,128)(2,1)} %collective-permute-done.2.r1_ref, bf16[2,424,256]{2,1,0:T(8,128)(2,1)} %collective-permute-done.1.e1_ref, ...), custom_call_target="tpu_custom_call" | custom-call | flops 2000683008 | bytes 10420224 | tf_op jit(solution)/shard_map/pallas_call | solution.py:20
  47.8 14.7 %all_to_all.10.sums_ref = f32[32,2,256]{2,1,0:T(2,128)S(1)} all-to-all(f32[32,2,256]{2,1,0:T(2,128)S(1)} %get-tuple-element.30), channel_id=1, replica_groups=mesh['frames'=4,'rows'=8] {'frames','rows'}, dimensions={0} | all-to-all | bytes 131072 | tf_op jit(solution)/shard_map/all_to_all | solution.py:260
  62.5 1.2 %shard_map.62 = bf16[1,4,424,256]{3,2,1,0:T(8,128)(2,1)} custom-call(f32[4,424,256]{2,1,0:T(8,128)S(1)} %get-tuple-element.29.grad_ref, bf16[4,424,256]{2,1,0:T(8,128)(2,1)S(1)} %get-tuple-element.25.x_ref, f32[8,256]{1,0:T(8,128)S(1)} %get-tuple-element.26.params_ref, f32[32,2,256]{2,1,0:T(2,128)S(1)} %all_to_all.10.sums_ref), custom_call_target="tpu_custom_call" | custom-call | flops 4341760 | bytes 3473408 | tf_op jit(solution)/shard_map/pallas_call | solution.py:20
Async XLA Ops:
  0.0 33.2 %collective-permute-start = (bf16[4,424,256]{2,1,0:T(8,128)(2,1)}, bf16[4,424,256]{2,1,0:T(8,128)(2,1)S(1)}, u32[]{:S(2)}, u32[]{:S(2)}) collective-permute-start(bf16[4,424,256]{2,1,0:T(8,128)(2,1)} %bitcast.3), channel_id=1, source_target_pairs={{8,0},{24,16},{9,1},{25,17},{10,2},{26,18},{11,3},{27,19},{12,4},{... | collective-permute-start | bytes 2605064 | tf_op jit(solution)/shard_map/ppermute | solution.py:257
  3.5 20.5 %collective-permute-start.1 = (bf16[2,424,256]{2,1,0:T(8,128)(2,1)}, bf16[2,424,256]{2,1,0:T(8,128)(2,1)}, u32[]{:S(2)}, u32[]{:S(2)}) collective-permute-start(bf16[2,424,256]{2,1,0:T(8,128)(2,1)} %get-tuple-element.18), channel_id=1, source_target_pairs={{16,0},{17,1},{18,2},{19,3},{20,4},{21,5},{22,6},{23,7}} | collective-permute-start | bytes 1302536 | tf_op jit(solution)/shard_map/ppermute | solution.py:257
  4.8 28.4 %collective-permute-start.4 = (bf16[2,424,256]{2,1,0:T(8,128)(2,1)}, bf16[2,424,256]{2,1,0:T(8,128)(2,1)}, u32[]{:S(2)}, u32[]{:S(2)}) collective-permute-start(bf16[2,424,256]{2,1,0:T(8,128)(2,1)} %get-tuple-element.19), channel_id=1, source_target_pairs={{16,8},{17,9},{18,10},{19,11},{20,12},{21,13},{22,14},{23,15}} | collective-permute-start | bytes 1302536 | tf_op jit(solution)/shard_map/ppermute | solution.py:257
  6.2 27.0 %collective-permute-start.5 = (bf16[2,424,256]{2,1,0:T(8,128)(2,1)}, bf16[2,424,256]{2,1,0:T(8,128)(2,1)}, u32[]{:S(2)}, u32[]{:S(2)}) collective-permute-start(bf16[2,424,256]{2,1,0:T(8,128)(2,1)} %get-tuple-element.19), channel_id=1, source_target_pairs={{16,0},{24,8},{17,1},{25,9},{18,2},{26,10},{19,3},{27,11},{20,4},{... | collective-permute-start | bytes 1302536 | tf_op jit(solution)/shard_map/ppermute | solution.py:257
  7.5 35.7 %collective-permute-start.3 = (bf16[2,424,256]{2,1,0:T(8,128)(2,1)}, bf16[2,424,256]{2,1,0:T(8,128)(2,1)}, u32[]{:S(2)}, u32[]{:S(2)}) collective-permute-start(bf16[2,424,256]{2,1,0:T(8,128)(2,1)} %get-tuple-element.18), channel_id=1, source_target_pairs={{24,8},{25,9},{26,10},{27,11},{28,12},{29,13},{30,14},{31,15}} | collective-permute-start | bytes 1302536 | tf_op jit(solution)/shard_map/ppermute | solution.py:257
  11.1 27.6 %all-to-all-start = ((f32[32,2,256]{2,1,0:T(2,128)}), f32[32,2,256]{2,1,0:T(2,128)S(1)}, u32[]{:S(2)}, u32[]{:S(2)}) async-start(f32[32,2,256]{2,1,0:T(2,128)} %shard_map.58), calls=%async_computation | async-start | bytes 131072 | tf_op jit(solution)/shard_map/all_to_all | solution.py:260
  24.0 19.2 %collective-permute-start.2 = (bf16[2,424,256]{2,1,0:T(8,128)(2,1)}, bf16[2,424,256]{2,1,0:T(8,128)(2,1)}, u32[]{:S(2)}, u32[]{:S(2)}) collective-permute-start(bf16[2,424,256]{2,1,0:T(8,128)(2,1)} %collective-permute-done.1.e1_ref), channel_id=1, source_target_pairs={{0,8},{1,9},{2,10},{3,11},{4,12},{5,13},{6,14},{7,15}} | collective-permute-start | bytes 1302536 | tf_op jit(solution)/shard_map/ppermute | solution.py:257
  37.2 6.0 %collective-permute-start.6 = (bf16[424,256]{1,0:T(8,128)(2,1)}, bf16[424,256]{1,0:T(8,128)(2,1)S(1)}, u32[]{:S(2)}, u32[]{:S(2)}) collective-permute-start(bf16[424,256]{1,0:T(8,128)(2,1)} %get-tuple-element.27), channel_id=1, source_target_pairs={{0,1},{1,0},{2,3},{3,2},{4,5},{5,4},{6,7},{7,6},{8,9},{9,8},{10,11... | collective-permute-start | bytes 651272 | tf_op jit(solution)/shard_map/ppermute | solution.py:257
  37.3 5.9 %collective-permute-start.7 = (bf16[424,256]{1,0:T(8,128)(2,1)}, bf16[424,256]{1,0:T(8,128)(2,1)}, u32[]{:S(2)}, u32[]{:S(2)}) collective-permute-start(bf16[424,256]{1,0:T(8,128)(2,1)} %get-tuple-element.28), channel_id=1, source_target_pairs={{1,2},{3,4},{5,6},{2,1},{4,3},{6,5},{9,10},{11,12},{13,14},{10,9},... | collective-permute-start | bytes 651272 | tf_op jit(solution)/shard_map/ppermute | solution.py:257
